TPU v7x, 512 devices: a whole 4x8x8 slice. The times are simulated.
512 devices in a mesh: expert: 64 (over x, y_hi, z), tensor: 8 (over y_lo, core).
Axes of the slice: x: 4, y: 8 (y_hi: 2, y_lo: 4; y = y_hi * 4 + y_lo), z: 8, core: 2. Of those that a mesh axis runs over, the one named last changes fastest.
Arguments:
- tokens: bfloat16 [1024, 3584], P('expert', 'tensor'), may hold values from -6 to 6
- grad_out: bfloat16 [1024, 3584], P('expert', 'tensor'), may hold values from -6 to 6
- gate_weights: bfloat16 [1024, 8], P('expert'), may hold values from 0.099609375 to 1
- routing: int32 [1024, 8], P('expert'), may hold values from 0 to 63, all different within a row; in each aligned block of 16 rows (0 to 15, 16 to 31, ...) at most 3 rows name the same one
- w_gate: bfloat16 [64, 3584, 1024], P('expert', None, 'tensor'), may hold values from -0.09375 to 0.09375
- w_up: bfloat16 [64, 3584, 1024], P('expert', None, 'tensor'), may hold values from -0.09375 to 0.09375
- w_down: bfloat16 [64, 1024, 3584], P('expert', 'tensor'), may hold values from -0.1875 to 0.1875
Outputs:
- grad_tokens: bfloat16 [1024, 3584], P('expert', 'tensor')
- grad_gate: bfloat16 [64, 3584, 1024], P('expert', None, 'tensor')
- grad_up: bfloat16 [64, 3584, 1024], P('expert', None, 'tensor')
Inputs may be any that keep to these rules, and one draw needn't show every extreme that they name: `routing`: each row names 8 different experts; within the rows of one device (aligned blocks of 16 rows) no expert is named by more than 3 rows.
All inputs are finite; a program needn't handle non-finite values.
Results may differ from a plain program's by a relative error of at most 0.014.
Values may be sent and summed in bfloat16 or wider, within the bound.
No kernel may reach another device: no remote copies, remote signals or barrier semaphores. Data moves between devices by JAX's collectives and lax.ppermute only.
A program may use at most 64 MiB of HBM per device.

v0:
```python
import functools

import jax
import jax.numpy as jnp
from jax import lax
from jax.experimental import pallas as pl
from jax.experimental.pallas import tpu as pltpu
from jax.sharding import Mesh, PartitionSpec as P

BF = jnp.bfloat16
F32 = jnp.float32
AXES = ("x", "yh", "z", "yl", "core")
LANES = 128
HALF = 64
VMEM_LIMIT = 16 * 1024 * 1024
STASH_ROWS = 40 * 1024
VMEM_ALL = 67043328
HBM = pl.BlockSpec(memory_space=pltpu.MemorySpace.HBM)


def axis_sizes(experts, tensor):
    if (experts, tensor) == (64, 8):
        return (4, 2, 8, 4, 2)
    assert experts % 2 == 0 and tensor == experts
    return (2, 1, experts // 2, tensor // 2, 2)


def pitch(rows):
    tiles = -(-rows // 8)
    return 8 * (tiles + 1 - tiles % 2)


class Plan:
    def __init__(self, sizes, tok_rows, picks, part_w):
        self.nx, self.nyh, self.nz, self.nyl, self.nc = sizes
        self.tok, self.picks, self.part_w = tok_rows, picks, part_w
        experts = self.nx * self.nyh * self.nz
        self.cap = 3 * tok_rows * picks // (2 * experts)
        self.nb = self.nyh * self.nyl
        assert self.nb == self.nz
        self.nq = self.nx * self.nb
        self.full = part_w // LANES
        assert part_w == self.full * LANES + HALF
        self.groups = 2 * self.full + 1
        self.lanes = self.nb * tok_rows
        self.c = self.nyh * self.cap
        self.grp = self.nb * self.cap
        self.rows = self.nq * self.c
        self.msg = self.groups * self.grp
        self.pitch = pitch(self.msg)
        self.ntail = self.nyl // 2
        self.pairs = (self.cap + 1) // 2
        self.tail = -(-max(self.ntail * self.c, self.pairs * self.nz) // 8) * 8
        self.ret = self.full * self.grp + self.tail
        self.ret_pitch = pitch(self.ret)
        self.half_d = self.nyl * part_w
        self.pre = self.groups * tok_rows + 2 * picks
        self.fin = (self.full + 1) * tok_rows

    def device(self, x, yh, z, yl, core):
        return (((x * self.nyh + yh) * self.nz + z) * self.nyl + yl) * self.nc + core

    def column_groups(self):
        xs, yhs, zs, yls = map(range, (self.nx, self.nyh, self.nz, self.nyl))
        first = [[self.device(x, h, z, l, 0) for h in yhs for l in yls] for x in xs for z in zs]
        second = [
            [self.device(x, h, z, l, 1) for z in zs] for x in xs for h in yhs for l in yls
        ]
        return first + second

    def plane_groups(self):
        xs, yhs, zs, yls = map(range, (self.nx, self.nyh, self.nz, self.nyl))
        first = [[self.device(x, h, z, l, 0) for x in xs for z in zs] for h in yhs for l in yls]
        second = [[self.device(x, h, z, l, 1) for x in xs for h in yhs for l in yls] for z in zs]
        return first + second


def iota(shape, dim):
    return lax.broadcasted_iota(jnp.int32, shape, dim)


def call(kernel, outs, args, scratch=(), flops=0, spaces=None, limit=VMEM_LIMIT, out_spec=None):
    vm = pl.BlockSpec(memory_space=pltpu.VMEM)
    spaces = spaces or {}
    size = sum(a.size * a.dtype.itemsize for a in args) + sum(
        jnp.dtype(o[1]).itemsize * functools.reduce(lambda a, b: a * b, o[0]) for o in outs
    )
    shapes = [jax.ShapeDtypeStruct(s, d) for s, d in outs]
    return pl.pallas_call(
        kernel,
        out_shape=shapes,
        in_specs=[spaces.get(k, vm) for k in range(len(args))],
        out_specs=[out_spec or vm] * len(outs),
        scratch_shapes=list(scratch),
        compiler_params=pltpu.CompilerParams(vmem_limit_bytes=limit),
        cost_estimate=pl.CostEstimate(flops=flops, bytes_accessed=size, transcendentals=0),
    )(*args)


def pack_kernel(p, *refs):
    out_ref, sems = refs[4], refs[9]
    x_ref, dy_ref, route_ref, gate_ref = refs[5:9]
    fetches = [
        pltpu.make_async_copy(refs[k], refs[5 + k], sems.at[k]) for k in range(4)
    ]
    for fetch in fetches:
        fetch.start()
    for fetch in fetches:
        fetch.wait()
    in_y = lax.axis_index("yh") * p.nyl + lax.axis_index("yl")
    block = jnp.where(lax.axis_index("core") == 0, in_y, lax.axis_index("z"))
    top = p.full * LANES
    low = (iota((HALF, LANES), 1) == iota((HALF, LANES), 0)).astype(BF)
    high = (iota((HALF, LANES), 1) == iota((HALF, LANES), 0) + HALF).astype(BF)
    mixed = jnp.dot(x_ref[:, top:], low, preferred_element_type=F32) + jnp.dot(
        dy_ref[:, top:], high, preferred_element_type=F32
    )
    lanes = (iota((p.tok, LANES), 1) == iota((p.tok, LANES), 0) + block * p.tok).astype(BF)
    meta = jnp.concatenate(
        [route_ref[...].astype(F32), gate_ref[...].astype(F32)], axis=0
    ).astype(BF)
    placed = jnp.dot(meta, lanes, preferred_element_type=F32).astype(BF)
    t = p.tok
    for b in range(p.nb):
        for j in range(p.full):
            out_ref[b, j * t : (j + 1) * t, :] = x_ref[:, j * LANES : (j + 1) * LANES]
            k = p.full + 1 + j
            out_ref[b, k * t : (k + 1) * t, :] = dy_ref[:, j * LANES : (j + 1) * LANES]
        out_ref[b, p.full * t : (p.full + 1) * t, :] = mixed.astype(BF)
        out_ref[b, p.groups * t :, :] = placed


def slot_target(p, first):
    r = iota((p.grp, p.lanes), 0)
    b = iota((p.grp, p.lanes), 1) // p.tok
    c = r % p.c
    in_y = jnp.where((r // p.c == b % p.nyl) & (c // p.cap == b // p.nyl), c % p.cap, -2)
    in_z = jnp.where(r % p.nz == b, r // p.nz, -2)
    return jnp.where(first, in_y, in_z).astype(F32)


def one_hot(p, ranks, target, weight=1.0):
    eq = ranks[:, None, :] == target[None, :, :]
    return jnp.where(eq, weight, 0.0).astype(F32).reshape(-1, p.lanes).astype(BF)


def dispatch_kernel(p, in_ref, out_ref, rank_ref):
    first = lax.axis_index("core") == 0
    yh, z = lax.axis_index("yh"), lax.axis_index("z")
    t = p.tok
    meta = in_ref[0, p.groups * t :, :].astype(F32)
    for b in range(1, p.nb):
        meta = meta + in_ref[b, p.groups * t :, :].astype(F32)
    q = iota((p.nq, p.lanes), 0)
    in_y = ((q // p.nz) * p.nyh + yh) * p.nz + q % p.nz
    in_z = (q // p.nyl) * p.nz + z
    expert = jnp.where(first, in_y, in_z).astype(F32)
    hit = jnp.zeros((p.nq, p.lanes), F32)
    gate = jnp.zeros((p.nq, p.lanes), F32)
    for k in range(p.picks):
        same = meta[k : k + 1, : p.lanes] == expert
        hit = hit + jnp.where(same, 1.0, 0.0)
        gate = gate + jnp.where(same, meta[p.picks + k : p.picks + k + 1, : p.lanes], 0.0)
    a, b = iota((p.lanes, p.lanes), 0), iota((p.lanes, p.lanes), 1)
    before = jnp.where((a < b) & (a // t == b // t), 1.0, 0.0).astype(BF)
    rank = jnp.dot(hit.astype(BF), before, preferred_element_type=F32)
    ranks = jnp.where(hit > 0.5, rank, -1.0)
    rank_ref[...] = ranks
    target = slot_target(p, first)
    pick = one_hot(p, ranks, target)
    gate = jnp.broadcast_to(gate[:, None, :], (p.nq, p.grp, p.lanes))
    scaled = one_hot(p, ranks, target, gate)
    left = iota((p.nq * p.grp, LANES), 1) < HALF
    for g in range(p.groups):
        feats = in_ref[:, g * t : (g + 1) * t, :].reshape(p.lanes, LANES)
        rows = jnp.dot(pick if g <= p.full else scaled, feats, preferred_element_type=F32)
        if g == p.full:
            both = jnp.dot(scaled, feats, preferred_element_type=F32)
            rows = jnp.where(left, rows, both)
        out_ref[:, g * p.grp : (g + 1) * p.grp, :] = rows.astype(BF).reshape(p.nq, p.grp, LANES)


def project_kernel(p, in_ref, wgu_ref, wd_hbm, x_ref, pre_ref, flat, dy, wd, sem):
    fetch = pltpu.make_async_copy(wd_hbm.at[: p.half_d], wd, sem)
    fetch.start()
    first = lax.axis_index("core") == 0

    def piece_in_y(group, yl):
        row = group * p.grp + yl * p.c
        return jnp.concatenate(
            [flat[pl.ds(row + c, p.nq, stride=p.pitch), :] for c in range(p.c)], axis=0
        )

    def blocks():
        for yh in range(p.nyh):
            for c in range(p.cap):
                for x in range(p.nx):
                    yield c, (x * p.nyh + yh) * p.nyl

    def piece_in_z(group, yl):
        rows = [(s + yl) * p.pitch + group * p.grp + c * p.nz for c, s in blocks()]
        return jnp.concatenate([flat[r : r + p.nz, :] for r in rows], axis=0)

    left = iota((p.rows, LANES), 1) < HALF

    def project(piece):
        for s in range(p.nq):
            flat[s * p.pitch : s * p.pitch + p.msg, :] = in_ref[s].astype(F32)
        for j in range(p.full):
            for yl in range(p.nyl):
                at = (j * p.nyl + yl) * LANES
                x_ref[:, at : at + LANES] = piece(j, yl).astype(BF)
                dy[:, at : at + LANES] = piece(p.full + 1 + j, yl).astype(BF)
        for u in range(p.ntail):
            at = (p.full * p.nyl + u) * LANES
            a = piece(p.full, 2 * u)
            b = piece(p.full, 2 * u + 1)
            x_ref[:, at : at + LANES] = jnp.where(left, a, pltpu.roll(b, HALF, 1)).astype(BF)
            dy[:, at : at + LANES] = jnp.where(left, pltpu.roll(a, HALF, 1), b).astype(BF)
        pre = jnp.dot(x_ref[...], wgu_ref[...], preferred_element_type=F32)
        fetch.wait()
        back = jnp.dot(dy[...], wd[...], preferred_element_type=F32)
        two, three = 2 * LANES, 3 * LANES
        pre_ref[:, :two] = pre[:, :two]
        pre_ref[:, two:three] = back[:, :LANES]
        pre_ref[:, three : three + two] = pre[:, two:]
        pre_ref[:, three + two :] = back[:, LANES:]

    @pl.when(first)
    def _():
        project(piece_in_y)

    @pl.when(jnp.logical_not(first))
    def _():
        project(piece_in_z)


def stash_kernel(in_ref, out_ref, sem):
    copy = pltpu.make_async_copy(in_ref, out_ref.at[: in_ref.shape[0]], sem)
    copy.start()
    copy.wait()


def back_kernel(p, pre_ref, got_ref, wgu_ref, out_ref, d_ref, flat):
    two, three = 2 * LANES, 3 * LANES
    nt = (((1,), (1,)), ((), ()))
    tail = p.full * p.grp
    chunks = p.full * p.nyl
    left = iota((p.nz, LANES), 1) < HALF
    for k in range(2):
        mine, theirs = k * three, (1 - k) * three

        def whole(at):
            own = pre_ref[:, mine + at : mine + at + LANES]
            return own + got_ref[:, theirs + at : theirs + at + LANES]

        pre_gate, pre_up, scaled = whole(0), whole(LANES), whole(two)
        sig = 1.0 / (1.0 + jnp.exp(-pre_gate))
        d_gate = scaled * pre_up * sig * (1.0 + pre_gate * (1.0 - sig))
        d_ref[:, k * two : k * two + LANES] = d_gate.astype(BF)
        d_ref[:, k * two + LANES : (k + 1) * two] = (scaled * pre_gate * sig).astype(BF)

    def part(k):
        at = k * LANES
        return lax.dot_general(
            d_ref[...], wgu_ref[at : at + LANES, :], nt, preferred_element_type=F32
        )

    def put_in_y(k, value):
        base = k * p.c if k < chunks else tail + (k - chunks) * p.c
        for c in range(p.c):
            flat[pl.ds(base + c, p.nq, stride=p.ret_pitch), :] = value[c * p.nq : (c + 1) * p.nq, :]

    def put_in_z(k, value):
        def block(yh, c, x):
            at = ((yh * p.cap + c) * p.nx + x) * p.nz
            return value[at : at + p.nz, :]

        for yh in range(p.nyh):
            for x in range(p.nx):
                s = (x * p.nyh + yh) * p.nyl
                if k < chunks:
                    for c in range(p.cap):
                        row = (s + k % p.nyl) * p.ret_pitch + k // p.nyl * p.grp + c * p.nz
                        flat[row : row + p.nz, :] = block(yh, c, x)
                    continue
                for c in range(0, p.cap, 2):
                    one = block(yh, c, x)
                    two = block(yh, c + 1, x) if c + 1 < p.cap else one
                    ends = (
                        jnp.where(left, one, pltpu.roll(two, HALF, 1)),
                        jnp.where(left, pltpu.roll(one, HALF, 1), two),
                    )
                    for h in range(2):
                        row = (s + 2 * (k - chunks) + h) * p.ret_pitch + tail + c // 2 * p.nz
                        flat[row : row + p.nz, :] = ends[h]

    def store():
        for s in range(p.nq):
            out_ref[s] = flat[s * p.ret_pitch : s * p.ret_pitch + p.ret, :].astype(BF)

    first = lax.axis_index("core") == 0

    @pl.when(first)
    def _():
        for r in range(tail + p.ntail * p.c, tail + p.tail):
            flat[pl.ds(r, p.nq, stride=p.ret_pitch), :] = jnp.zeros((p.nq, LANES), F32)
        for k in range(chunks + p.ntail):
            put_in_y(k, part(k))
        store()

    @pl.when(jnp.logical_not(first))
    def _():
        for k in range(chunks + p.ntail):
            put_in_z(k, part(k))
        store()


def combine_kernel(p, in_ref, rank_ref, out_ref):
    t = p.tok
    tn = (((0,), (0,)), ((), ()))
    first = lax.axis_index("core") == 0
    pick = one_hot(p, rank_ref[...], slot_target(p, first))

    def total(g):
        rows = in_ref[:, g * p.grp : (g + 1) * p.grp, :].reshape(p.nq * p.grp, LANES)
        return lax.dot_general(pick, rows, tn, preferred_element_type=F32)

    for g in range(p.full):
        out_ref[:, g * t : (g + 1) * t, :] = total(g).astype(BF).reshape(p.nb, t, LANES)
    tail = p.full * p.grp
    pick = pick.reshape(p.nq, p.grp, p.lanes)

    def tail_total(start, stop, at):
        rows = in_ref[:, tail + at : tail + at + stop - start, :].reshape(-1, LANES)
        chosen = pick[:, start:stop, :].reshape(-1, p.lanes)
        return lax.dot_general(chosen, rows, tn, preferred_element_type=F32)

    @pl.when(first)
    def _():
        last = tail_total(0, p.tail, 0)
        for b in range(p.nb):
            src = (b // p.nyl) * p.nyl + (b % p.nyl) // 2
            out_ref[b, p.full * t :, :] = last[src * t : (src + 1) * t, :].astype(BF)

    @pl.when(jnp.logical_not(first))
    def _():
        sides = [None, None]
        for c in range(p.cap):
            part = tail_total(c * p.nz, (c + 1) * p.nz, c // 2 * p.nz)
            sides[c % 2] = part if sides[c % 2] is None else sides[c % 2] + part
        last = sides[0] + pltpu.roll(sides[1], HALF, 1)
        out_ref[:, p.full * t :, :] = last.astype(BF).reshape(p.nb, t, LANES)


def finish_kernel(p, in_ref, out_ref):
    odd = jnp.where(lax.axis_index("core") == 0, lax.axis_index("yl") % 2, 0)
    total = in_ref[0].astype(F32)
    for b in range(1, p.nb):
        total = total + in_ref[b].astype(F32)
    t = p.tok
    for j in range(p.full):
        out_ref[:, j * LANES : (j + 1) * LANES] = total[j * t : (j + 1) * t, :].astype(BF)
    tail = total[p.full * t :, :]
    tail = jnp.where(odd == 1, pltpu.roll(tail, HALF, 1), tail)
    out_ref[:, p.full * LANES :] = tail[:, :HALF].astype(BF)


def grads_kernel(p, x_ref, d_ref, mine_ref, other_ref):
    tn = (((0,), (0,)), ((), ()))

    def put(yl, at, size, src, got, k):
        mine_ref[k, yl, at : at + size, :] = got[src : src + size, k * LANES : (k + 1) * LANES]

    def put_other(yl, at, size, src, got):
        other_ref[yl, at : at + size, :] = got[src : src + size, :]

    for k in range(p.full * p.nyl + p.ntail):
        x = x_ref[:, k * LANES : (k + 1) * LANES]
        both = lax.dot_general(x, d_ref[...], tn, preferred_element_type=F32).astype(BF)
        mine, other = both[:, : 2 * LANES], both[:, 2 * LANES :]
        if k < p.full * p.nyl:
            spots = [(k % p.nyl, (k // p.nyl) * LANES, LANES, 0)]
        else:
            u = k - p.full * p.nyl
            spots = [(2 * u + h, p.full * LANES, HALF, h * HALF) for h in range(2)]
        for spot in spots:
            put(*spot, mine, 0)
            put(*spot, mine, 1)
            put_other(*spot, other)


def assemble_kernel(p, mine_ref, got_ref, gate_ref, up_ref):
    core = lax.axis_index("core")
    for yl in range(p.nyl):
        gate_ref[yl, core] = mine_ref[0, yl]
        up_ref[yl, core] = mine_ref[1, yl]
        gate_ref[yl, 1 - core] = got_ref[yl, :, :LANES]
        up_ref[yl, 1 - core] = got_ref[yl, :, LANES:]


def lane_tiles(p, w):
    top = p.full * LANES
    n = w.shape[-1]
    tiles = w[:, :top].reshape(p.nyl, p.full, LANES, n).transpose(1, 0, 2, 3).reshape(-1, n)
    return jnp.concatenate([tiles, w[:, top:].reshape(-1, n)], axis=0)


def body(sizes, *args):
    return program(sizes, *args)


def program(sizes, tokens, grad_out, gate_weights, routing, w_gate, w_up, w_down):
    p = Plan(sizes, *routing.shape, tokens.shape[1])
    swap = [(0, 1), (1, 0)]
    core = lax.axis_index("core")
    bind = functools.partial

    def exchange(v):
        return lax.ppermute(v, "core", swap)

    def all_to_all(v, groups):
        return lax.all_to_all(
            v, AXES, split_axis=0, concat_axis=0, axis_index_groups=groups, tiled=True
        )

    column_groups, plane_groups = p.column_groups(), p.plane_groups()

    (pre,) = call(
        bind(pack_kernel, p),
        [((p.nb, p.pre, LANES), BF)],
        (tokens, grad_out, routing.T, gate_weights.T),
        scratch=[
            pltpu.VMEM(tokens.shape, BF),
            pltpu.VMEM(grad_out.shape, BF),
            pltpu.VMEM(routing.shape[::-1], routing.dtype),
            pltpu.VMEM(gate_weights.shape[::-1], BF),
            pltpu.SemaphoreType.DMA((4,)),
        ],
        spaces={k: HBM for k in range(4)},
        limit=VMEM_ALL,
    )
    column = all_to_all(pre, column_groups)

    w_gate, w_up, w_down = lax.optimization_barrier((w_gate, w_up, w_down, pre))[:3]
    shape = (p.nyl, p.nc, p.part_w, LANES)
    weights = jnp.stack(
        [w_gate[0].reshape(shape), w_up[0].reshape(shape), w_down[0].T.reshape(shape)]
    )
    mine = lax.dynamic_index_in_dim(weights, core, axis=2, keepdims=False)
    other = lax.dynamic_index_in_dim(weights, 1 - core, axis=2, keepdims=False)
    theirs = exchange(other)
    wgu = lane_tiles(p, jnp.concatenate([mine[0], mine[1], theirs[0], theirs[1]], axis=-1))
    wd = lane_tiles(p, jnp.concatenate([mine[2], theirs[2]], axis=-1))
    (wd,) = call(
        stash_kernel,
        [((STASH_ROWS, 2 * LANES), BF)],
        (wd,),
        scratch=[pltpu.SemaphoreType.DMA],
        out_spec=HBM,
        limit=3 * VMEM_LIMIT,
    )

    sent, ranks = call(
        bind(dispatch_kernel, p), [((p.nq, p.msg, LANES), BF), ((p.nq, p.lanes), F32)], (column,)
    )
    received = all_to_all(sent, plane_groups)
    rows_x, partial = call(
        bind(project_kernel, p),
        [
            ((p.rows, p.half_d), BF),
            ((p.rows, 6 * LANES), F32),
        ],
        (received, wgu, wd),
        scratch=[
            pltpu.VMEM((p.nq * p.pitch, LANES), F32),
            pltpu.VMEM((p.rows, p.half_d), BF),
            pltpu.VMEM((p.half_d, 2 * LANES), BF),
            pltpu.SemaphoreType.DMA,
        ],
        spaces={2: HBM},
        limit=3 * VMEM_LIMIT,
    )
    back, d_all = call(
        bind(back_kernel, p),
        [((p.nq, p.ret, LANES), BF), ((p.rows, 4 * LANES), BF)],
        (partial, exchange(partial), wgu),
        scratch=[pltpu.VMEM((p.nq * p.ret_pitch, LANES), F32)],
    )
    returned = all_to_all(back, plane_groups)
    rows_x, d_all = lax.optimization_barrier((rows_x, d_all, back))[:2]
    grad_mine, grad_other = call(
        bind(grads_kernel, p),
        [((2, p.nyl, p.part_w, LANES), BF), ((p.nyl, p.part_w, 2 * LANES), BF)],
        (rows_x, d_all),
    )
    grad_got = exchange(grad_other)
    (share,) = call(bind(combine_kernel, p), [((p.nb, p.fin, LANES), BF)], (returned, ranks))
    last = all_to_all(share, column_groups)
    grad_mine, grad_got = lax.optimization_barrier((grad_mine, grad_got, share))[:2]
    grad_g, grad_u = call(
        bind(assemble_kernel, p), [(shape, BF), (shape, BF)], (grad_mine, grad_got)
    )
    (grad_tokens,) = call(bind(finish_kernel, p), [((p.tok, p.part_w), BF)], (last,))
    out = (1, p.nyl * p.nc * p.part_w, LANES)
    return grad_tokens, grad_g.reshape(out), grad_u.reshape(out)


def solution(mesh):
    sizes = axis_sizes(mesh.shape["expert"], mesh.shape["tensor"])
    inner = Mesh(mesh.devices.reshape(sizes), AXES)
    ex, te = AXES[:3], AXES[3:]
    placed = (
        P(ex, te),
        P(ex, te),
        P(ex, None),
        P(ex, None),
        P(ex, None, te),
        P(ex, None, te),
        P(ex, te, None),
    )
    return jax.shard_map(
        functools.partial(body, sizes),
        mesh=inner,
        in_specs=placed,
        out_specs=(P(ex, te), P(ex, None, te), P(ex, None, te)),
        check_vma=False,
    )
```

profile of v0, /device:TPU:64, one launch (start us, length us, event | category | flops | bytes accessed | tf_op | source)
XLA Modules:
  0.0 99.5 jit_solution(6774570468777857658)
XLA Ops:
  0.6 1.6 %shard_map.94 = bf16[8,128,128]{2,1,0:T(8,128)(2,1)} custom-call(bf16[16,448]{1,0:T(8,128)(2,1)} %refs_0_.1, bf16[16,448]{1,0:T(8,128)(2,1)} %refs_1_.1, s32[8,16]{1,0:T(8,128)} %bitcast.46, bf16[8,16]{1,0:T(8,128)(2,1)} %bitcast.47), custom_call_target="tpu_custom_call" | custom-call | bytes 291584 | tf_op jit(solution)/shard_map/pallas_call | solution.py:89
  2.3 0.0 copy-start.3
  2.3 0.0 copy-start.4
  2.3 7.2 %all-to-all-start = ((bf16[8,128,128]{2,1,0:T(8,128)(2,1)}), bf16[8,128,128]{2,1,0:T(8,128)(2,1)S(1)}, u32[]{:S(2)}, u32[]{:S(2)}) async-start(bf16[8,128,128]{2,1,0:T(8,128)(2,1)} %shard_map.94), calls=%async_computation | async-start | bytes 524288 | tf_op jit(solution)/shard_map/all_to_all | solution.py:423
  9.5 1.5 %copy.15 = bf16[1,128,3584]{1,2,0:T(8,128)(2,1)S(1)} copy(bf16[1,128,3584]{2,1,0:T(8,128)(2,1)} %param.13) | data formatting | bytes 1835008 | tf_op jit(solution)/shard_map/optimization_barrier | solution.py:445
  11.1 0.0 copy-done.3
  11.1 0.0 copy-done.4
  11.1 0.3 pad_maximum_fusion
  11.4 0.0 copy-start.2
  11.4 1.4 %dynamic-slice_bitcast_fusion.1 = (bf16[3,4,1,448,128]{4,3,1,2,0:T(8,128)(2,1)S(1)}, bf16[3,4,448,128]{3,2,1,0:T(8,128)(2,1)}) fusion(bf16[3,4,2,448,128]{4,3,2,1,0:T(8,128)(2,1)S(1)} %pad_maximum_fusion, s32[]{:T(128)S(6)} %select_n.7, s32[]{:T(128)S(6)} %select_n.8), kind=kLoop, calls=%fused_computation.4 | loop fusion | bytes 5505032 | tf_op jit(solution)/shard_map/jit(dynamic_index_in_dim)/dynamic_slice | solution.py:450
  12.8 0.5 copy-done.2
  13.4 4.0 %collective-permute-start = (bf16[3,4,448,128]{3,2,1,0:T(8,128)(2,1)}, bf16[3,4,448,128]{3,2,1,0:T(8,128)(2,1)}, u32[]{:S(2)}, u32[]{:S(2)}) collective-permute-start(bf16[3,4,448,128]{3,2,1,0:T(8,128)(2,1)} %get-tuple-element.38), channel_id=1, source_target_pairs={{0,1},{1,0},{2,3},{3,2},{4,5},{5,4},{6,7},{7,6},{8,9},{9,8},{10,11... | collective-permute-start | bytes 4128776 | tf_op jit(solution)/shard_map/ppermute | solution.py:420
  17.4 2.6 %all-to-all-done.in_ref = bf16[8,128,128]{2,1,0:T(8,128)(2,1)S(1)} async-done(((bf16[8,128,128]{2,1,0:T(8,128)(2,1)}), bf16[8,128,128]{2,1,0:T(8,128)(2,1)S(1)}, u32[]{:S(2)}, u32[]{:S(2)}) %all-to-all-start) | async-done | bytes 262176 | tf_op jit(solution)/shard_map/all_to_all | solution.py:423
  20.0 1.9 %shard_map.95 = (bf16[32,168,128]{2,1,0:T(8,128)(2,1)}, f32[32,128]{1,0:T(8,128)S(1)}) custom-call(bf16[8,128,128]{2,1,0:T(8,128)(2,1)S(1)} %all-to-all-done.in_ref), custom_call_target="tpu_custom_call" | custom-call | bytes 1654784 | tf_op jit(solution)/shard_map/pallas_call | solution.py:89
  21.9 12.6 %all-to-all-start.1 = ((bf16[32,168,128]{2,1,0:T(8,128)(2,1)}), bf16[32,168,128]{2,1,0:T(8,128)(2,1)S(1)}, u32[]{:S(2)}, u32[]{:S(2)}) async-start(bf16[32,168,128]{2,1,0:T(8,128)(2,1)} %get-tuple-element.20), calls=%async_computation.1 | async-start | bytes 2752512 | tf_op jit(solution)/shard_map/all_to_all | solution.py:423
  34.5 1.1 %dynamic-slice_bitcast_fusion.2 = bf16[4,448,128]{2,1,0:T(8,128)(2,1)S(1)} fusion(bf16[3,4,2,448,128]{4,3,2,1,0:T(8,128)(2,1)} %copy-done.2, s32[]{:T(128)S(6)} %add.10, s32[]{:T(128)S(6)} %select_n.7), kind=kLoop, calls=%fused_computation.10 | loop fusion | bytes 917512 | tf_op jit(solution)/shard_map/squeeze | solution.py:454
  35.5 0.1 slice_bitcast_fusion.4
  35.6 0.0 collective-permute-done
  35.6 1.4 %slice_bitcast_fusion = (bf16[4,448,128]{2,1,0:T(8,128)(2,1)S(1)}, bf16[4,448,128]{2,1,0:T(8,128)(2,1)S(1)}, bf16[4,448,128]{2,1,0:T(8,128)(2,1)S(1)}) fusion(bf16[3,4,448,128]{3,2,1,0:T(8,128)(2,1)} %collective-permute-done), kind=kLoop, calls=%fused_computation.9 | loop fusion | bytes 2752512 | tf_op jit(solution)/shard_map/squeeze | solution.py:454
  37.0 0.1 fusion
  37.1 0.1 copy.19
  37.2 0.2 pad_maximum_fusion.1
  37.4 0.1 slice.47
  37.5 0.1 copy.18
  37.6 0.1 pad_maximum_fusion.3.in_ref
  37.7 0.9 shard_map.96.wd_hbm
  38.7 0.1 pad_maximum_fusion.2.wgu_ref
  38.8 17.9 %all-to-all-done.1.in_ref = bf16[32,168,128]{2,1,0:T(8,128)(2,1)S(1)} async-done(((bf16[32,168,128]{2,1,0:T(8,128)(2,1)}), bf16[32,168,128]{2,1,0:T(8,128)(2,1)S(1)}, u32[]{:S(2)}, u32[]{:S(2)}) %all-to-all-start.1) | async-done | bytes 1376288 | tf_op jit(solution)/shard_map/all_to_all | solution.py:423
  56.7 1.8 %shard_map.97 = (bf16[192,1792]{1,0:T(8,128)(2,1)S(1)}, f32[192,768]{1,0:T(8,128)S(1)}) custom-call(bf16[32,168,128]{2,1,0:T(8,128)(2,1)S(1)} %all-to-all-done.1.in_ref, bf16[1792,512]{1,0:T(8,128)(2,1)S(1)} %pad_maximum_fusion.2.wgu_ref, bf16[40960,256]{1,0:T(8,128)(2,1)} %shard_map.96.wd_hbm), custom_call_target="tpu_custom_call" | custom-call | bytes 25460736 | tf_op jit(solution)/shard_map/pallas_call | solution.py:89
  58.5 0.0 copy-start
  58.5 1.9 %collective-permute-start.1 = (f32[192,768]{1,0:T(8,128)S(1)}, f32[192,768]{1,0:T(8,128)S(1)}, u32[]{:S(2)}, u32[]{:S(2)}) collective-permute-start(f32[192,768]{1,0:T(8,128)S(1)} %get-tuple-element.24.pre_ref), channel_id=1, source_target_pairs={{0,1},{1,0},{2,3},{3,2},{4,5},{5,4},{6,7},{7,6},{8,9},{9,8},{10,11... | collective-permute-start | bytes 1769480 | tf_op jit(solution)/shard_map/ppermute | solution.py:420
  60.4 2.0 %collective-permute-done.1.got_ref = f32[192,768]{1,0:T(8,128)S(1)} collective-permute-done((f32[192,768]{1,0:T(8,128)S(1)}, f32[192,768]{1,0:T(8,128)S(1)}, u32[]{:S(2)}, u32[]{:S(2)}) %collective-permute-start.1) | collective-permute-done | bytes 589856 | tf_op jit(solution)/shard_map/ppermute | solution.py:420
  62.4 1.9 %shard_map.98 = (bf16[32,88,128]{2,1,0:T(8,128)(2,1)}, bf16[192,512]{1,0:T(8,128)(2,1)S(1)}) custom-call(f32[192,768]{1,0:T(8,128)S(1)} %get-tuple-element.24.pre_ref, f32[192,768]{1,0:T(8,128)S(1)} %collective-permute-done.1.got_ref, bf16[1792,512]{1,0:T(8,128)(2,1)S(1)} %pad_maximum_fusion.2.wgu_ref), custom_call_target="tpu_custom_call" | custom-call | bytes 3932160 | tf_op jit(solution)/shard_map/pallas_call | solution.py:89
  64.3 0.0 copy-done
  64.3 0.0 copy-start.1
  64.3 5.4 %all-to-all-start.2 = ((bf16[32,88,128]{2,1,0:T(8,128)(2,1)}), bf16[32,88,128]{2,1,0:T(8,128)(2,1)S(1)}, u32[]{:S(2)}, u32[]{:S(2)}) async-start(bf16[32,88,128]{2,1,0:T(8,128)(2,1)} %get-tuple-element.25), calls=%async_computation.2 | async-start | bytes 1441792 | tf_op jit(solution)/shard_map/all_to_all | solution.py:423
  69.7 0.0 copy-done.1
  69.7 1.6 %shard_map.101 = (bf16[2,4,448,128]{3,2,1,0:T(8,128)(2,1)S(1)}, bf16[4,448,256]{2,1,0:T(8,128)(2,1)}) custom-call(bf16[192,1792]{1,0:T(8,128)(2,1)S(1)} %copy-done.1, bf16[192,512]{1,0:T(8,128)(2,1)S(1)} %get-tuple-element.30.d_ref), custom_call_target="tpu_custom_call" | custom-call | bytes 2719744 | tf_op jit(solution)/shard_map/pallas_call | solution.py:89
  71.3 1.9 %collective-permute-start.2 = (bf16[4,448,256]{2,1,0:T(8,128)(2,1)}, bf16[4,448,256]{2,1,0:T(8,128)(2,1)S(1)}, u32[]{:S(2)}, u32[]{:S(2)}) collective-permute-start(bf16[4,448,256]{2,1,0:T(8,128)(2,1)} %get-tuple-element.32), channel_id=1, source_target_pairs={{0,1},{1,0},{2,3},{3,2},{4,5},{5,4},{6,7},{7,6},{8,9},{9,8},{10,11... | collective-permute-start | bytes 2752520 | tf_op jit(solution)/shard_map/ppermute | solution.py:420
  73.2 11.9 %all-to-all-done.2.in_ref = bf16[32,88,128]{2,1,0:T(8,128)(2,1)S(1)} async-done(((bf16[32,88,128]{2,1,0:T(8,128)(2,1)}), bf16[32,88,128]{2,1,0:T(8,128)(2,1)S(1)}, u32[]{:S(2)}, u32[]{:S(2)}) %all-to-all-start.2) | async-done | bytes 720928 | tf_op jit(solution)/shard_map/all_to_all | solution.py:423
  85.2 1.3 %shard_map.99 = bf16[8,64,128]{2,1,0:T(8,128)(2,1)} custom-call(bf16[32,88,128]{2,1,0:T(8,128)(2,1)S(1)} %all-to-all-done.2.in_ref, f32[32,128]{1,0:T(8,128)S(1)} %get-tuple-element.26.rank_ref), custom_call_target="tpu_custom_call" | custom-call | bytes 868352 | tf_op jit(solution)/shard_map/pallas_call | solution.py:89
  86.4 3.4 %all-to-all-start.3 = ((bf16[8,64,128]{2,1,0:T(8,128)(2,1)}), bf16[8,64,128]{2,1,0:T(8,128)(2,1)S(1)}, u32[]{:S(2)}, u32[]{:S(2)}) async-start(bf16[8,64,128]{2,1,0:T(8,128)(2,1)} %shard_map.99), calls=%async_computation.3 | async-start | bytes 262144 | tf_op jit(solution)/shard_map/all_to_all | solution.py:423
  89.8 0.0 collective-permute-done.2.got_ref
  89.8 1.4 %shard_map.102 = (bf16[4,2,448,128]{3,2,1,0:T(8,128)(2,1)}, bf16[4,2,448,128]{3,2,1,0:T(8,128)(2,1)}) custom-call(bf16[2,4,448,128]{3,2,1,0:T(8,128)(2,1)S(1)} %get-tuple-element.33.mine_ref, bf16[4,448,256]{2,1,0:T(8,128)(2,1)S(1)} %collective-permute-done.2.got_ref), custom_call_target="tpu_custom_call" | custom-call | bytes 3670016 | tf_op jit(solution)/shard_map/pallas_call | solution.py:89
  91.3 7.5 %all-to-all-done.3.in_ref = bf16[8,64,128]{2,1,0:T(8,128)(2,1)S(1)} async-done(((bf16[8,64,128]{2,1,0:T(8,128)(2,1)}), bf16[8,64,128]{2,1,0:T(8,128)(2,1)S(1)}, u32[]{:S(2)}, u32[]{:S(2)}) %all-to-all-start.3) | async-done | bytes 131104 | tf_op jit(solution)/shard_map/all_to_all | solution.py:423
  98.8 0.7 shard_map.100
  (2 shorter events, 0.1 us)
Async XLA Ops:
  2.3 8.8 %copy-start.3 = (bf16[1,3584,128]{2,1,0:T(8,128)(2,1)S(1)}, bf16[1,3584,128]{2,1,0:T(8,128)(2,1)}, u32[]{:S(2)}) copy-start(bf16[1,3584,128]{2,1,0:T(8,128)(2,1)} %param.12) | copy-start | bytes 2752516
  2.3 8.8 %copy-start.4 = (bf16[1,3584,128]{2,1,0:T(8,128)(2,1)S(1)}, bf16[1,3584,128]{2,1,0:T(8,128)(2,1)}, u32[]{:S(2)}) copy-start(bf16[1,3584,128]{2,1,0:T(8,128)(2,1)} %param.11) | copy-start | bytes 2752516
  2.3 17.7 %all-to-all-start = ((bf16[8,128,128]{2,1,0:T(8,128)(2,1)}), bf16[8,128,128]{2,1,0:T(8,128)(2,1)S(1)}, u32[]{:S(2)}, u32[]{:S(2)}) async-start(bf16[8,128,128]{2,1,0:T(8,128)(2,1)} %shard_map.94), calls=%async_computation | async-start | bytes 524288 | tf_op jit(solution)/shard_map/all_to_all | solution.py:423
  11.4 1.9 %copy-start.2 = (bf16[3,4,2,448,128]{4,3,2,1,0:T(8,128)(2,1)}, bf16[3,4,2,448,128]{4,3,2,1,0:T(8,128)(2,1)S(1)}, u32[]{:S(2)}) copy-start(bf16[3,4,2,448,128]{4,3,2,1,0:T(8,128)(2,1)S(1)} %pad_maximum_fusion) | copy-start | bytes 8257540
  13.4 22.2 %collective-permute-start = (bf16[3,4,448,128]{3,2,1,0:T(8,128)(2,1)}, bf16[3,4,448,128]{3,2,1,0:T(8,128)(2,1)}, u32[]{:S(2)}, u32[]{:S(2)}) collective-permute-start(bf16[3,4,448,128]{3,2,1,0:T(8,128)(2,1)} %get-tuple-element.38), channel_id=1, source_target_pairs={{0,1},{1,0},{2,3},{3,2},{4,5},{5,4},{6,7},{7,6},{8,9},{9,8},{10,11... | collective-permute-start | bytes 4128776 | tf_op jit(solution)/shard_map/ppermute | solution.py:420
  21.9 34.8 %all-to-all-start.1 = ((bf16[32,168,128]{2,1,0:T(8,128)(2,1)}), bf16[32,168,128]{2,1,0:T(8,128)(2,1)S(1)}, u32[]{:S(2)}, u32[]{:S(2)}) async-start(bf16[32,168,128]{2,1,0:T(8,128)(2,1)} %get-tuple-element.20), calls=%async_computation.1 | async-start | bytes 2752512 | tf_op jit(solution)/shard_map/all_to_all | solution.py:423
  58.5 5.8 %copy-start = (bf16[192,1792]{1,0:T(8,128)(2,1)}, bf16[192,1792]{1,0:T(8,128)(2,1)S(1)}, u32[]{:S(2)}) copy-start(bf16[192,1792]{1,0:T(8,128)(2,1)S(1)} %get-tuple-element.29.x_ref) | copy-start | bytes 2064388
  58.5 3.9 %collective-permute-start.1 = (f32[192,768]{1,0:T(8,128)S(1)}, f32[192,768]{1,0:T(8,128)S(1)}, u32[]{:S(2)}, u32[]{:S(2)}) collective-permute-start(f32[192,768]{1,0:T(8,128)S(1)} %get-tuple-element.24.pre_ref), channel_id=1, source_target_pairs={{0,1},{1,0},{2,3},{3,2},{4,5},{5,4},{6,7},{7,6},{8,9},{9,8},{10,11... | collective-permute-start | bytes 1769480 | tf_op jit(solution)/shard_map/ppermute | solution.py:420
  64.3 5.4 %copy-start.1 = (bf16[192,1792]{1,0:T(8,128)(2,1)S(1)}, bf16[192,1792]{1,0:T(8,128)(2,1)}, u32[]{:S(2)}) copy-start(bf16[192,1792]{1,0:T(8,128)(2,1)} %copy-done) | copy-start | bytes 2064388
  64.3 20.9 %all-to-all-start.2 = ((bf16[32,88,128]{2,1,0:T(8,128)(2,1)}), bf16[32,88,128]{2,1,0:T(8,128)(2,1)S(1)}, u32[]{:S(2)}, u32[]{:S(2)}) async-start(bf16[32,88,128]{2,1,0:T(8,128)(2,1)} %get-tuple-element.25), calls=%async_computation.2 | async-start | bytes 1441792 | tf_op jit(solution)/shard_map/all_to_all | solution.py:423
  71.3 18.5 %collective-permute-start.2 = (bf16[4,448,256]{2,1,0:T(8,128)(2,1)}, bf16[4,448,256]{2,1,0:T(8,128)(2,1)S(1)}, u32[]{:S(2)}, u32[]{:S(2)}) collective-permute-start(bf16[4,448,256]{2,1,0:T(8,128)(2,1)} %get-tuple-element.32), channel_id=1, source_target_pairs={{0,1},{1,0},{2,3},{3,2},{4,5},{5,4},{6,7},{7,6},{8,9},{9,8},{10,11... | collective-permute-start | bytes 2752520 | tf_op jit(solution)/shard_map/ppermute | solution.py:420
  86.4 12.4 %all-to-all-start.3 = ((bf16[8,64,128]{2,1,0:T(8,128)(2,1)}), bf16[8,64,128]{2,1,0:T(8,128)(2,1)S(1)}, u32[]{:S(2)}, u32[]{:S(2)}) async-start(bf16[8,64,128]{2,1,0:T(8,128)(2,1)} %shard_map.99), calls=%async_computation.3 | async-start | bytes 262144 | tf_op jit(solution)/shard_map/all_to_all | solution.py:423
where the time goes:
time: 100 us; the launch traced here: 99.5 us
  waiting for transfers between devices  42 us (42%)
  starting transfers between devices  36.5 us (36%)
  Pallas kernels  13.1 us (13%)
  local copies, waits for them, and re-layouts  6.28 us (6%)
    all_to_all x4, waiting for transfers between devices, all_to_all(): lax.all_to_all(v, AXES, split_axis=0, concat_axis=0, axis_index_groups=gr...  40 us
    all_to_all x4, starting transfers between devices, all_to_all(): lax.all_to_all(v, AXES, split_axis=0, concat_axis=0, axis_index_groups=gr...  28.6 us
    pallas_call x9, Pallas kernels, call(): pl.pallas_call(kernel, out_shape=shapes, in_specs=[spaces.get(k, vm) for...  13.1 us
    ppermute x3, starting transfers between devices, exchange(): return lax.ppermute(v, 'core', swap)  7.86 us
    squeeze x2, local copies, waits for them, and re-layouts, program(): wd = lane_tiles(p, jnp.concatenate([mine[2], theirs[2]], axis=-1))  2.45 us
  transfers between devices with their start and end apart: 7, of which 5 were waited for; matrix products, arithmetic and copies ran while one was open for 7% of the time, Pallas kernels for 7%

commit v1 on v0

--- a/solution.py
+++ b/solution.py
@@ -79,7 +79,7 @@
     return lax.broadcasted_iota(jnp.int32, shape, dim)
 
 
-def call(kernel, outs, args, scratch=(), flops=0, spaces=None, limit=VMEM_LIMIT, out_spec=None):
+def call(kernel, outs, args, scratch=(), flops=0, spaces=None, limit=VMEM_LIMIT, out_spaces=None):
     vm = pl.BlockSpec(memory_space=pltpu.VMEM)
     spaces = spaces or {}
     size = sum(a.size * a.dtype.itemsize for a in args) + sum(
@@ -90,7 +90,7 @@
         kernel,
         out_shape=shapes,
         in_specs=[spaces.get(k, vm) for k in range(len(args))],
-        out_specs=[out_spec or vm] * len(outs),
+        out_specs=[(out_spaces or {}).get(k, vm) for k in range(len(outs))],
         scratch_shapes=list(scratch),
         compiler_params=pltpu.CompilerParams(vmem_limit_bytes=limit),
         cost_estimate=pl.CostEstimate(flops=flops, bytes_accessed=size, transcendentals=0),
@@ -98,7 +98,7 @@
 
 
 def pack_kernel(p, *refs):
-    out_ref, sems = refs[4], refs[9]
+    out_ref, block_ref, sems = refs[4], refs[9], refs[10]
     x_ref, dy_ref, route_ref, gate_ref = refs[5:9]
     fetches = [
         pltpu.make_async_copy(refs[k], refs[5 + k], sems.at[k]) for k in range(4)
@@ -121,13 +121,19 @@
     ).astype(BF)
     placed = jnp.dot(meta, lanes, preferred_element_type=F32).astype(BF)
     t = p.tok
-    for b in range(p.nb):
-        for j in range(p.full):
-            out_ref[b, j * t : (j + 1) * t, :] = x_ref[:, j * LANES : (j + 1) * LANES]
-            k = p.full + 1 + j
-            out_ref[b, k * t : (k + 1) * t, :] = dy_ref[:, j * LANES : (j + 1) * LANES]
-        out_ref[b, p.full * t : (p.full + 1) * t, :] = mixed.astype(BF)
-        out_ref[b, p.groups * t :, :] = placed
+    for j in range(p.full):
+        block_ref[j * t : (j + 1) * t, :] = x_ref[:, j * LANES : (j + 1) * LANES]
+        k = p.full + 1 + j
+        block_ref[k * t : (k + 1) * t, :] = dy_ref[:, j * LANES : (j + 1) * LANES]
+    block_ref[p.full * t : (p.full + 1) * t, :] = mixed.astype(BF)
+    block_ref[p.groups * t :, :] = placed
+    stores = [
+        pltpu.make_async_copy(block_ref, out_ref.at[b], sems.at[4 + b]) for b in range(p.nb)
+    ]
+    for store in stores:
+        store.start()
+    for store in stores:
+        store.wait()
 
 
 def slot_target(p, first):
@@ -144,7 +150,7 @@
     return jnp.where(eq, weight, 0.0).astype(F32).reshape(-1, p.lanes).astype(BF)
 
 
-def dispatch_kernel(p, in_ref, out_ref, rank_ref):
+def dispatch_kernel(p, in_ref, out_ref, rank_ref, held, sems):
     first = lax.axis_index("core") == 0
     yh, z = lax.axis_index("yh"), lax.axis_index("z")
     t = p.tok
@@ -171,13 +177,20 @@
     gate = jnp.broadcast_to(gate[:, None, :], (p.nq, p.grp, p.lanes))
     scaled = one_hot(p, ranks, target, gate)
     left = iota((p.nq * p.grp, LANES), 1) < HALF
+    stores = []
     for g in range(p.groups):
         feats = in_ref[:, g * t : (g + 1) * t, :].reshape(p.lanes, LANES)
         rows = jnp.dot(pick if g <= p.full else scaled, feats, preferred_element_type=F32)
         if g == p.full:
             both = jnp.dot(scaled, feats, preferred_element_type=F32)
             rows = jnp.where(left, rows, both)
-        out_ref[:, g * p.grp : (g + 1) * p.grp, :] = rows.astype(BF).reshape(p.nq, p.grp, LANES)
+        at = slice(g * p.grp, (g + 1) * p.grp)
+        held[:, at, :] = rows.astype(BF).reshape(p.nq, p.grp, LANES)
+        store = pltpu.make_async_copy(held.at[:, at, :], out_ref.at[:, at, :], sems.at[g])
+        store.start()
+        stores.append(store)
+    for store in stores:
+        store.wait()
 
 
 def project_kernel(p, in_ref, wgu_ref, wd_hbm, x_ref, pre_ref, flat, dy, wd, sem):
@@ -241,11 +254,12 @@
     copy.wait()
 
 
-def back_kernel(p, pre_ref, got_ref, wgu_ref, out_ref, d_ref, flat):
+def back_kernel(p, pre_ref, got_ref, wgu_ref, out_ref, d_ref, flat, held, sems):
     two, three = 2 * LANES, 3 * LANES
     nt = (((1,), (1,)), ((), ()))
     tail = p.full * p.grp
     chunks = p.full * p.nyl
+    parts = 4
     left = iota((p.nz, LANES), 1) < HALF
     for k in range(2):
         mine, theirs = k * three, (1 - k) * three
@@ -296,8 +310,15 @@
                         flat[row : row + p.nz, :] = ends[h]
 
     def store():
-        for s in range(p.nq):
-            out_ref[s] = flat[s * p.ret_pitch : s * p.ret_pitch + p.ret, :].astype(BF)
+        copies = []
+        for k in range(parts):
+            at = slice(k * p.nq // parts, (k + 1) * p.nq // parts)
+            for s in range(at.start, at.stop):
+                held[s] = flat[s * p.ret_pitch : s * p.ret_pitch + p.ret, :].astype(BF)
+            copies.append(pltpu.make_async_copy(held.at[at], out_ref.at[at], sems.at[k]))
+            copies[-1].start()
+        for copy in copies:
+            copy.wait()
 
     first = lax.axis_index("core") == 0
 
@@ -316,29 +337,22 @@
         store()
 
 
-def combine_kernel(p, in_ref, rank_ref, out_ref):
+def combine_kernel(p, in_ref, pick_ref, ends_ref, out_ref):
     t = p.tok
-    tn = (((0,), (0,)), ((), ()))
     first = lax.axis_index("core") == 0
-    pick = one_hot(p, rank_ref[...], slot_target(p, first))
-
-    def total(g):
+    for g in range(p.full):
         rows = in_ref[:, g * p.grp : (g + 1) * p.grp, :].reshape(p.nq * p.grp, LANES)
-        return lax.dot_general(pick, rows, tn, preferred_element_type=F32)
-
-    for g in range(p.full):
-        out_ref[:, g * t : (g + 1) * t, :] = total(g).astype(BF).reshape(p.nb, t, LANES)
+        total = jnp.dot(pick_ref[...], rows, preferred_element_type=F32)
+        out_ref[:, g * t : (g + 1) * t, :] = total.astype(BF).reshape(p.nb, t, LANES)
     tail = p.full * p.grp
-    pick = pick.reshape(p.nq, p.grp, p.lanes)
-
-    def tail_total(start, stop, at):
-        rows = in_ref[:, tail + at : tail + at + stop - start, :].reshape(-1, LANES)
-        chosen = pick[:, start:stop, :].reshape(-1, p.lanes)
-        return lax.dot_general(chosen, rows, tn, preferred_element_type=F32)
+
+    def tail_total(lanes, start, rows):
+        rows = in_ref[:, tail + start : tail + start + rows, :].reshape(-1, LANES)
+        return jnp.dot(ends_ref[:, lanes], rows, preferred_element_type=F32)
 
     @pl.when(first)
     def _():
-        last = tail_total(0, p.tail, 0)
+        last = tail_total(slice(0, p.nq * p.tail), 0, p.tail)
         for b in range(p.nb):
             src = (b // p.nyl) * p.nyl + (b % p.nyl) // 2
             out_ref[b, p.full * t :, :] = last[src * t : (src + 1) * t, :].astype(BF)
@@ -346,8 +360,9 @@
     @pl.when(jnp.logical_not(first))
     def _():
         sides = [None, None]
+        n = p.nq * p.nz
         for c in range(p.cap):
-            part = tail_total(c * p.nz, (c + 1) * p.nz, c // 2 * p.nz)
+            part = tail_total(slice(c * n, (c + 1) * n), c // 2 * p.nz, p.nz)
             sides[c % 2] = part if sides[c % 2] is None else sides[c % 2] + part
         last = sides[0] + pltpu.roll(sides[1], HALF, 1)
         out_ref[:, p.full * t :, :] = last.astype(BF).reshape(p.nb, t, LANES)
@@ -366,7 +381,26 @@
     out_ref[:, p.full * LANES :] = tail[:, :HALF].astype(BF)
 
 
-def grads_kernel(p, x_ref, d_ref, mine_ref, other_ref):
+def grads_kernel(p, x_ref, d_ref, rank_ref, mine_ref, other_ref, pick_ref, ends_ref):
+    first = lax.axis_index("core") == 0
+    eq = rank_ref[...][:, None, :] == slot_target(p, first)[None, :, :]
+    pick = jnp.where(eq, 1.0, 0.0).astype(F32)
+
+    def turned(rows):
+        return rows.reshape(-1, p.lanes).T.astype(BF)
+
+    pick_ref[...] = turned(pick)
+
+    @pl.when(first)
+    def _():
+        ends_ref[:, : p.nq * p.tail] = turned(pick[:, : p.tail, :])
+
+    @pl.when(jnp.logical_not(first))
+    def _():
+        n = p.nq * p.nz
+        for c in range(p.cap):
+            ends_ref[:, c * n : (c + 1) * n] = turned(pick[:, c * p.nz : (c + 1) * p.nz, :])
+
     tn = (((0,), (0,)), ((), ()))
 
     def put(yl, at, size, src, got, k):
@@ -435,8 +469,10 @@
             pltpu.VMEM(grad_out.shape, BF),
             pltpu.VMEM(routing.shape[::-1], routing.dtype),
             pltpu.VMEM(gate_weights.shape[::-1], BF),
-            pltpu.SemaphoreType.DMA((4,)),
+            pltpu.VMEM((p.pre, LANES), BF),
+            pltpu.SemaphoreType.DMA((4 + p.nb,)),
         ],
+        out_spaces={0: HBM},
         spaces={k: HBM for k in range(4)},
         limit=VMEM_ALL,
     )
@@ -457,12 +493,19 @@
         [((STASH_ROWS, 2 * LANES), BF)],
         (wd,),
         scratch=[pltpu.SemaphoreType.DMA],
-        out_spec=HBM,
+        out_spaces={0: HBM},
         limit=3 * VMEM_LIMIT,
     )
 
     sent, ranks = call(
-        bind(dispatch_kernel, p), [((p.nq, p.msg, LANES), BF), ((p.nq, p.lanes), F32)], (column,)
+        bind(dispatch_kernel, p),
+        [((p.nq, p.msg, LANES), BF), ((p.nq, p.lanes), F32)],
+        (column,),
+        scratch=[
+            pltpu.VMEM((p.nq, p.msg, LANES), BF),
+            pltpu.SemaphoreType.DMA((p.groups,)),
+        ],
+        out_spaces={0: HBM},
     )
     received = all_to_all(sent, plane_groups)
     rows_x, partial = call(
@@ -473,7 +516,7 @@
         ],
         (received, wgu, wd),
         scratch=[
-            pltpu.VMEM((p.nq * p.pitch, LANES), F32),
+            pltpu.VMEM(((p.nq + 1) * p.pitch, LANES), F32),
             pltpu.VMEM((p.rows, p.half_d), BF),
             pltpu.VMEM((p.half_d, 2 * LANES), BF),
             pltpu.SemaphoreType.DMA,
@@ -485,17 +528,23 @@
         bind(back_kernel, p),
         [((p.nq, p.ret, LANES), BF), ((p.rows, 4 * LANES), BF)],
         (partial, exchange(partial), wgu),
-        scratch=[pltpu.VMEM((p.nq * p.ret_pitch, LANES), F32)],
+        scratch=[
+            pltpu.VMEM(((p.nq + 1) * p.ret_pitch, LANES), F32),
+            pltpu.VMEM((p.nq, p.ret, LANES), BF),
+            pltpu.SemaphoreType.DMA((4,)),
+        ],
+        out_spaces={0: HBM},
     )
     returned = all_to_all(back, plane_groups)
     rows_x, d_all = lax.optimization_barrier((rows_x, d_all, back))[:2]
-    grad_mine, grad_other = call(
+    chosen = ((p.lanes, p.nq * p.grp), BF)
+    grad_mine, grad_other, pick, ends = call(
         bind(grads_kernel, p),
-        [((2, p.nyl, p.part_w, LANES), BF), ((p.nyl, p.part_w, 2 * LANES), BF)],
-        (rows_x, d_all),
+        [((2, p.nyl, p.part_w, LANES), BF), ((p.nyl, p.part_w, 2 * LANES), BF), chosen, chosen],
+        (rows_x, d_all, ranks),
     )
     grad_got = exchange(grad_other)
-    (share,) = call(bind(combine_kernel, p), [((p.nb, p.fin, LANES), BF)], (returned, ranks))
+    (share,) = call(bind(combine_kernel, p), [((p.nb, p.fin, LANES), BF)], (returned, pick, ends))
     last = all_to_all(share, column_groups)
     grad_mine, grad_got = lax.optimization_barrier((grad_mine, grad_got, share))[:2]
     grad_g, grad_u = call(

time: 100 us -> 100 us (level)
  no operation moved by 1% of the time
where the time goes in v1:
time: 100 us; the launch traced here: 99.3 us
  waiting for transfers between devices  41.7 us (42%)
  starting transfers between devices  36.5 us (36%)
  Pallas kernels  13.1 us (13%)
  local copies, waits for them, and re-layouts  6.27 us (6%)
    all_to_all x4, waiting for transfers between devices, all_to_all(): lax.all_to_all(v, AXES, split_axis=0, concat_axis=0, axis_index_groups=gr...  39.8 us
    all_to_all x4, starting transfers between devices, all_to_all(): lax.all_to_all(v, AXES, split_axis=0, concat_axis=0, axis_index_groups=gr...  28.6 us
    pallas_call x9, Pallas kernels, call(): pl.pallas_call(kernel, out_shape=shapes, in_specs=[spaces.get(k, vm) for...  13.1 us
    ppermute x3, starting transfers between devices, exchange(): return lax.ppermute(v, 'core', swap)  7.87 us
    squeeze x2, local copies, waits for them, and re-layouts, program(): wd = lane_tiles(p, jnp.concatenate([mine[2], theirs[2]], axis=-1))  2.45 us
  transfers between devices with their start and end apart: 7, of which 5 were waited for; matrix products, arithmetic and copies ran while one was open for 7% of the time, Pallas kernels for 7%

profile of v1, /device:TPU:64, one launch (start us, length us, event | category | flops | bytes accessed | tf_op | source)
XLA Modules:
  0.0 99.3 jit_solution(15486744508339661823)
XLA Ops:
  0.6 1.7 %shard_map.94 = bf16[8,128,128]{2,1,0:T(8,128)(2,1)} custom-call(bf16[16,448]{1,0:T(8,128)(2,1)} %refs_0_.1, bf16[16,448]{1,0:T(8,128)(2,1)} %refs_1_.1, s32[8,16]{1,0:T(8,128)} %bitcast.46, bf16[8,16]{1,0:T(8,128)(2,1)} %bitcast.47), custom_call_target="tpu_custom_call" | custom-call | bytes 291584 | tf_op jit(solution)/shard_map/pallas_call | solution.py:89
  2.3 0.0 copy-start.3
  2.3 0.0 copy-start.4
  2.3 7.2 %all-to-all-start = ((bf16[8,128,128]{2,1,0:T(8,128)(2,1)}), bf16[8,128,128]{2,1,0:T(8,128)(2,1)S(1)}, u32[]{:S(2)}, u32[]{:S(2)}) async-start(bf16[8,128,128]{2,1,0:T(8,128)(2,1)} %shard_map.94), calls=%async_computation | async-start | bytes 524288 | tf_op jit(solution)/shard_map/all_to_all | solution.py:457
  9.6 1.5 %copy.15 = bf16[1,128,3584]{1,2,0:T(8,128)(2,1)S(1)} copy(bf16[1,128,3584]{2,1,0:T(8,128)(2,1)} %param.13) | data formatting | bytes 1835008 | tf_op jit(solution)/shard_map/optimization_barrier | solution.py:481
  11.1 0.0 copy-done.3
  11.1 0.0 copy-done.4
  11.2 0.3 pad_maximum_fusion
  11.5 0.0 copy-start.2
  11.5 1.5 %dynamic-slice_bitcast_fusion.1 = (bf16[3,4,1,448,128]{4,3,1,2,0:T(8,128)(2,1)S(1)}, bf16[3,4,448,128]{3,2,1,0:T(8,128)(2,1)}) fusion(bf16[3,4,2,448,128]{4,3,2,1,0:T(8,128)(2,1)S(1)} %pad_maximum_fusion, s32[]{:T(128)S(6)} %select_n.7, s32[]{:T(128)S(6)} %select_n.8), kind=kLoop, calls=%fused_computation.4 | loop fusion | bytes 5505032 | tf_op jit(solution)/shard_map/jit(dynamic_index_in_dim)/dynamic_slice | solution.py:486
  13.0 0.4 copy-done.2
  13.4 4.0 %collective-permute-start = (bf16[3,4,448,128]{3,2,1,0:T(8,128)(2,1)}, bf16[3,4,448,128]{3,2,1,0:T(8,128)(2,1)}, u32[]{:S(2)}, u32[]{:S(2)}) collective-permute-start(bf16[3,4,448,128]{3,2,1,0:T(8,128)(2,1)} %get-tuple-element.42), channel_id=1, source_target_pairs={{0,1},{1,0},{2,3},{3,2},{4,5},{5,4},{6,7},{7,6},{8,9},{9,8},{10,11... | collective-permute-start | bytes 4128776 | tf_op jit(solution)/shard_map/ppermute | solution.py:454
  17.4 2.6 %all-to-all-done.in_ref = bf16[8,128,128]{2,1,0:T(8,128)(2,1)S(1)} async-done(((bf16[8,128,128]{2,1,0:T(8,128)(2,1)}), bf16[8,128,128]{2,1,0:T(8,128)(2,1)S(1)}, u32[]{:S(2)}, u32[]{:S(2)}) %all-to-all-start) | async-done | bytes 262176 | tf_op jit(solution)/shard_map/all_to_all | solution.py:457
  20.1 1.7 %shard_map.95 = (bf16[32,168,128]{2,1,0:T(8,128)(2,1)}, f32[32,128]{1,0:T(8,128)S(1)}) custom-call(bf16[8,128,128]{2,1,0:T(8,128)(2,1)S(1)} %all-to-all-done.in_ref), custom_call_target="tpu_custom_call" | custom-call | bytes 1654784 | tf_op jit(solution)/shard_map/pallas_call | solution.py:89
  21.7 12.6 %all-to-all-start.1 = ((bf16[32,168,128]{2,1,0:T(8,128)(2,1)}), bf16[32,168,128]{2,1,0:T(8,128)(2,1)S(1)}, u32[]{:S(2)}, u32[]{:S(2)}) async-start(bf16[32,168,128]{2,1,0:T(8,128)(2,1)} %get-tuple-element.22), calls=%async_computation.1 | async-start | bytes 2752512 | tf_op jit(solution)/shard_map/all_to_all | solution.py:457
  34.3 1.1 %dynamic-slice_bitcast_fusion.2 = bf16[4,448,128]{2,1,0:T(8,128)(2,1)S(1)} fusion(bf16[3,4,2,448,128]{4,3,2,1,0:T(8,128)(2,1)} %copy-done.2, s32[]{:T(128)S(6)} %add.10, s32[]{:T(128)S(6)} %select_n.7), kind=kLoop, calls=%fused_computation.10 | loop fusion | bytes 917512 | tf_op jit(solution)/shard_map/squeeze | solution.py:490
  35.4 0.1 slice_bitcast_fusion.4
  35.5 0.0 collective-permute-done
  35.5 1.4 %slice_bitcast_fusion = (bf16[4,448,128]{2,1,0:T(8,128)(2,1)S(1)}, bf16[4,448,128]{2,1,0:T(8,128)(2,1)S(1)}, bf16[4,448,128]{2,1,0:T(8,128)(2,1)S(1)}) fusion(bf16[3,4,448,128]{3,2,1,0:T(8,128)(2,1)} %collective-permute-done), kind=kLoop, calls=%fused_computation.9 | loop fusion | bytes 2752512 | tf_op jit(solution)/shard_map/squeeze | solution.py:490
  36.9 0.1 fusion
  37.0 0.1 copy.19
  37.0 0.2 pad_maximum_fusion.1
  37.2 0.1 slice.47
  37.4 0.1 copy.18
  37.5 0.1 pad_maximum_fusion.3.in_ref
  37.6 0.9 shard_map.96.wd_hbm
  38.6 0.1 pad_maximum_fusion.2.wgu_ref
  38.7 17.9 %all-to-all-done.1.in_ref = bf16[32,168,128]{2,1,0:T(8,128)(2,1)S(1)} async-done(((bf16[32,168,128]{2,1,0:T(8,128)(2,1)}), bf16[32,168,128]{2,1,0:T(8,128)(2,1)S(1)}, u32[]{:S(2)}, u32[]{:S(2)}) %all-to-all-start.1) | async-done | bytes 1376288 | tf_op jit(solution)/shard_map/all_to_all | solution.py:457
  56.6 1.8 %shard_map.97 = (bf16[192,1792]{1,0:T(8,128)(2,1)S(1)}, f32[192,768]{1,0:T(8,128)S(1)}) custom-call(bf16[32,168,128]{2,1,0:T(8,128)(2,1)S(1)} %all-to-all-done.1.in_ref, bf16[1792,512]{1,0:T(8,128)(2,1)S(1)} %pad_maximum_fusion.2.wgu_ref, bf16[40960,256]{1,0:T(8,128)(2,1)} %shard_map.96.wd_hbm), custom_call_target="tpu_custom_call" | custom-call | bytes 25460736 | tf_op jit(solution)/shard_map/pallas_call | solution.py:89
  58.4 0.0 copy-start
  58.4 1.9 %collective-permute-start.1 = (f32[192,768]{1,0:T(8,128)S(1)}, f32[192,768]{1,0:T(8,128)S(1)}, u32[]{:S(2)}, u32[]{:S(2)}) collective-permute-start(f32[192,768]{1,0:T(8,128)S(1)} %get-tuple-element.26.pre_ref), channel_id=1, source_target_pairs={{0,1},{1,0},{2,3},{3,2},{4,5},{5,4},{6,7},{7,6},{8,9},{9,8},{10,11... | collective-permute-start | bytes 1769480 | tf_op jit(solution)/shard_map/ppermute | solution.py:454
  60.3 2.0 %collective-permute-done.1.got_ref = f32[192,768]{1,0:T(8,128)S(1)} collective-permute-done((f32[192,768]{1,0:T(8,128)S(1)}, f32[192,768]{1,0:T(8,128)S(1)}, u32[]{:S(2)}, u32[]{:S(2)}) %collective-permute-start.1) | collective-permute-done | bytes 589856 | tf_op jit(solution)/shard_map/ppermute | solution.py:454
  62.3 1.9 %shard_map.98 = (bf16[32,88,128]{2,1,0:T(8,128)(2,1)}, bf16[192,512]{1,0:T(8,128)(2,1)S(1)}) custom-call(f32[192,768]{1,0:T(8,128)S(1)} %get-tuple-element.26.pre_ref, f32[192,768]{1,0:T(8,128)S(1)} %collective-permute-done.1.got_ref, bf16[1792,512]{1,0:T(8,128)(2,1)S(1)} %pad_maximum_fusion.2.wgu_ref), custom_call_target="tpu_custom_call" | custom-call | bytes 3932160 | tf_op jit(solution)/shard_map/pallas_call | solution.py:89
  64.2 0.0 copy-done
  64.2 0.0 copy-start.1
  64.2 5.4 %all-to-all-start.2 = ((bf16[32,88,128]{2,1,0:T(8,128)(2,1)}), bf16[32,88,128]{2,1,0:T(8,128)(2,1)S(1)}, u32[]{:S(2)}, u32[]{:S(2)}) async-start(bf16[32,88,128]{2,1,0:T(8,128)(2,1)} %get-tuple-element.27), calls=%async_computation.2 | async-start | bytes 1441792 | tf_op jit(solution)/shard_map/all_to_all | solution.py:457
  69.6 0.0 copy-done.1
  69.6 1.9 %shard_map.99 = (bf16[2,4,448,128]{3,2,1,0:T(8,128)(2,1)S(1)}, bf16[4,448,256]{2,1,0:T(8,128)(2,1)}, bf16[128,768]{1,0:T(8,128)(2,1)S(1)}, bf16[128,768]{1,0:T(8,128)(2,1)S(1)}) custom-call(bf16[192,1792]{1,0:T(8,128)(2,1)S(1)} %copy-done.1, bf16[192,512]{1,0:T(8,128)(2,1)S(1)} %get-tuple-element.31.d_ref, f32[32,128]{1,0:T(8,128)S(1)} %get-tuple-element.32.rank_ref), custom_call_target="tpu_custom_call" | custom-call | bytes 3129344 | tf_op jit(solution)/shard_map/pallas_call | solution.py:89
  71.5 1.9 %collective-permute-start.2 = (bf16[4,448,256]{2,1,0:T(8,128)(2,1)}, bf16[4,448,256]{2,1,0:T(8,128)(2,1)S(1)}, u32[]{:S(2)}, u32[]{:S(2)}) collective-permute-start(bf16[4,448,256]{2,1,0:T(8,128)(2,1)} %get-tuple-element.36), channel_id=1, source_target_pairs={{0,1},{1,0},{2,3},{3,2},{4,5},{5,4},{6,7},{7,6},{8,9},{9,8},{10,11... | collective-permute-start | bytes 2752520 | tf_op jit(solution)/shard_map/ppermute | solution.py:454
  73.4 11.7 %all-to-all-done.2.in_ref = bf16[32,88,128]{2,1,0:T(8,128)(2,1)S(1)} async-done(((bf16[32,88,128]{2,1,0:T(8,128)(2,1)}), bf16[32,88,128]{2,1,0:T(8,128)(2,1)S(1)}, u32[]{:S(2)}, u32[]{:S(2)}) %all-to-all-start.2) | async-done | bytes 720928 | tf_op jit(solution)/shard_map/all_to_all | solution.py:457
  85.1 1.1 %shard_map.100 = bf16[8,64,128]{2,1,0:T(8,128)(2,1)} custom-call(bf16[32,88,128]{2,1,0:T(8,128)(2,1)S(1)} %all-to-all-done.2.in_ref, bf16[128,768]{1,0:T(8,128)(2,1)S(1)} %get-tuple-element.33.pick_ref, bf16[128,768]{1,0:T(8,128)(2,1)S(1)} %get-tuple-element.34.ends_ref), custom_call_target="tpu_custom_call" | custom-call | bytes 1245184 | tf_op jit(solution)/shard_map/pallas_call | solution.py:89
  86.2 3.4 %all-to-all-start.3 = ((bf16[8,64,128]{2,1,0:T(8,128)(2,1)}), bf16[8,64,128]{2,1,0:T(8,128)(2,1)S(1)}, u32[]{:S(2)}, u32[]{:S(2)}) async-start(bf16[8,64,128]{2,1,0:T(8,128)(2,1)} %shard_map.100), calls=%async_computation.3 | async-start | bytes 262144 | tf_op jit(solution)/shard_map/all_to_all | solution.py:457
  89.6 0.0 collective-permute-done.2.got_ref
  89.6 1.4 %shard_map.102 = (bf16[4,2,448,128]{3,2,1,0:T(8,128)(2,1)}, bf16[4,2,448,128]{3,2,1,0:T(8,128)(2,1)}) custom-call(bf16[2,4,448,128]{3,2,1,0:T(8,128)(2,1)S(1)} %get-tuple-element.37.mine_ref, bf16[4,448,256]{2,1,0:T(8,128)(2,1)S(1)} %collective-permute-done.2.got_ref), custom_call_target="tpu_custom_call" | custom-call | bytes 3670016 | tf_op jit(solution)/shard_map/pallas_call | solution.py:89
  91.1 7.5 %all-to-all-done.3.in_ref = bf16[8,64,128]{2,1,0:T(8,128)(2,1)S(1)} async-done(((bf16[8,64,128]{2,1,0:T(8,128)(2,1)}), bf16[8,64,128]{2,1,0:T(8,128)(2,1)S(1)}, u32[]{:S(2)}, u32[]{:S(2)}) %all-to-all-start.3) | async-done | bytes 131104 | tf_op jit(solution)/shard_map/all_to_all | solution.py:457
  98.6 0.7 shard_map.101
  (2 shorter events, 0.1 us)
Async XLA Ops:
  2.3 8.8 %copy-start.3 = (bf16[1,3584,128]{2,1,0:T(8,128)(2,1)S(1)}, bf16[1,3584,128]{2,1,0:T(8,128)(2,1)}, u32[]{:S(2)}) copy-start(bf16[1,3584,128]{2,1,0:T(8,128)(2,1)} %param.12) | copy-start | bytes 2752516
  2.3 8.8 %copy-start.4 = (bf16[1,3584,128]{2,1,0:T(8,128)(2,1)S(1)}, bf16[1,3584,128]{2,1,0:T(8,128)(2,1)}, u32[]{:S(2)}) copy-start(bf16[1,3584,128]{2,1,0:T(8,128)(2,1)} %param.11) | copy-start | bytes 2752516
  2.3 17.7 %all-to-all-start = ((bf16[8,128,128]{2,1,0:T(8,128)(2,1)}), bf16[8,128,128]{2,1,0:T(8,128)(2,1)S(1)}, u32[]{:S(2)}, u32[]{:S(2)}) async-start(bf16[8,128,128]{2,1,0:T(8,128)(2,1)} %shard_map.94), calls=%async_computation | async-start | bytes 524288 | tf_op jit(solution)/shard_map/all_to_all | solution.py:457
  11.5 1.9 %copy-start.2 = (bf16[3,4,2,448,128]{4,3,2,1,0:T(8,128)(2,1)}, bf16[3,4,2,448,128]{4,3,2,1,0:T(8,128)(2,1)S(1)}, u32[]{:S(2)}) copy-start(bf16[3,4,2,448,128]{4,3,2,1,0:T(8,128)(2,1)S(1)} %pad_maximum_fusion) | copy-start | bytes 8257540
  13.4 22.1 %collective-permute-start = (bf16[3,4,448,128]{3,2,1,0:T(8,128)(2,1)}, bf16[3,4,448,128]{3,2,1,0:T(8,128)(2,1)}, u32[]{:S(2)}, u32[]{:S(2)}) collective-permute-start(bf16[3,4,448,128]{3,2,1,0:T(8,128)(2,1)} %get-tuple-element.42), channel_id=1, source_target_pairs={{0,1},{1,0},{2,3},{3,2},{4,5},{5,4},{6,7},{7,6},{8,9},{9,8},{10,11... | collective-permute-start | bytes 4128776 | tf_op jit(solution)/shard_map/ppermute | solution.py:454
  21.7 34.9 %all-to-all-start.1 = ((bf16[32,168,128]{2,1,0:T(8,128)(2,1)}), bf16[32,168,128]{2,1,0:T(8,128)(2,1)S(1)}, u32[]{:S(2)}, u32[]{:S(2)}) async-start(bf16[32,168,128]{2,1,0:T(8,128)(2,1)} %get-tuple-element.22), calls=%async_computation.1 | async-start | bytes 2752512 | tf_op jit(solution)/shard_map/all_to_all | solution.py:457
  58.4 5.8 %copy-start = (bf16[192,1792]{1,0:T(8,128)(2,1)}, bf16[192,1792]{1,0:T(8,128)(2,1)S(1)}, u32[]{:S(2)}) copy-start(bf16[192,1792]{1,0:T(8,128)(2,1)S(1)} %get-tuple-element.30.x_ref) | copy-start | bytes 2064388
  58.4 3.9 %collective-permute-start.1 = (f32[192,768]{1,0:T(8,128)S(1)}, f32[192,768]{1,0:T(8,128)S(1)}, u32[]{:S(2)}, u32[]{:S(2)}) collective-permute-start(f32[192,768]{1,0:T(8,128)S(1)} %get-tuple-element.26.pre_ref), channel_id=1, source_target_pairs={{0,1},{1,0},{2,3},{3,2},{4,5},{5,4},{6,7},{7,6},{8,9},{9,8},{10,11... | collective-permute-start | bytes 1769480 | tf_op jit(solution)/shard_map/ppermute | solution.py:454
  64.2 5.4 %copy-start.1 = (bf16[192,1792]{1,0:T(8,128)(2,1)S(1)}, bf16[192,1792]{1,0:T(8,128)(2,1)}, u32[]{:S(2)}) copy-start(bf16[192,1792]{1,0:T(8,128)(2,1)} %copy-done) | copy-start | bytes 2064388
  64.2 20.9 %all-to-all-start.2 = ((bf16[32,88,128]{2,1,0:T(8,128)(2,1)}), bf16[32,88,128]{2,1,0:T(8,128)(2,1)S(1)}, u32[]{:S(2)}, u32[]{:S(2)}) async-start(bf16[32,88,128]{2,1,0:T(8,128)(2,1)} %get-tuple-element.27), calls=%async_computation.2 | async-start | bytes 1441792 | tf_op jit(solution)/shard_map/all_to_all | solution.py:457
  71.5 18.1 %collective-permute-start.2 = (bf16[4,448,256]{2,1,0:T(8,128)(2,1)}, bf16[4,448,256]{2,1,0:T(8,128)(2,1)S(1)}, u32[]{:S(2)}, u32[]{:S(2)}) collective-permute-start(bf16[4,448,256]{2,1,0:T(8,128)(2,1)} %get-tuple-element.36), channel_id=1, source_target_pairs={{0,1},{1,0},{2,3},{3,2},{4,5},{5,4},{6,7},{7,6},{8,9},{9,8},{10,11... | collective-permute-start | bytes 2752520 | tf_op jit(solution)/shard_map/ppermute | solution.py:454
  86.2 12.4 %all-to-all-start.3 = ((bf16[8,64,128]{2,1,0:T(8,128)(2,1)}), bf16[8,64,128]{2,1,0:T(8,128)(2,1)S(1)}, u32[]{:S(2)}, u32[]{:S(2)}) async-start(bf16[8,64,128]{2,1,0:T(8,128)(2,1)} %shard_map.100), calls=%async_computation.3 | async-start | bytes 262144 | tf_op jit(solution)/shard_map/all_to_all | solution.py:457

commit v2 on v1

--- a/solution.py
+++ b/solution.py
@@ -193,7 +193,7 @@
         store.wait()
 
 
-def project_kernel(p, in_ref, wgu_ref, wd_hbm, x_ref, pre_ref, flat, dy, wd, sem):
+def project_kernel(p, in_ref, wgu_ref, wd_hbm, x_ref, pre_ref, send_ref, flat, dy, wd, sem):
     fetch = pltpu.make_async_copy(wd_hbm.at[: p.half_d], wd, sem)
     fetch.start()
     first = lax.axis_index("core") == 0
@@ -238,6 +238,7 @@
         pre_ref[:, two:three] = back[:, :LANES]
         pre_ref[:, three : three + two] = pre[:, two:]
         pre_ref[:, three + two :] = back[:, LANES:]
+        send_ref[...] = pre_ref[...].astype(BF)
 
     @pl.when(first)
     def _():
@@ -259,14 +260,13 @@
     nt = (((1,), (1,)), ((), ()))
     tail = p.full * p.grp
     chunks = p.full * p.nyl
-    parts = 4
     left = iota((p.nz, LANES), 1) < HALF
     for k in range(2):
         mine, theirs = k * three, (1 - k) * three
 
         def whole(at):
             own = pre_ref[:, mine + at : mine + at + LANES]
-            return own + got_ref[:, theirs + at : theirs + at + LANES]
+            return own + got_ref[:, theirs + at : theirs + at + LANES].astype(F32)
 
         pre_gate, pre_up, scaled = whole(0), whole(LANES), whole(two)
         sig = 1.0 / (1.0 + jnp.exp(-pre_gate))
@@ -309,14 +309,27 @@
                         row = (s + 2 * (k - chunks) + h) * p.ret_pitch + tail + c // 2 * p.nz
                         flat[row : row + p.nz, :] = ends[h]
 
-    def store():
+    def rows_of(g):
+        return slice(g * p.grp, (g + 1) * p.grp if g < p.full else p.ret)
+
+    def store(g):
+        at = rows_of(g)
+        for s in range(p.nq):
+            base = s * p.ret_pitch
+            held[s, at, :] = flat[base + at.start : base + at.stop, :].astype(BF)
+        copy = pltpu.make_async_copy(held.at[:, at, :], out_ref.at[:, at, :], sems.at[g])
+        copy.start()
+        return copy
+
+    def run(put):
         copies = []
-        for k in range(parts):
-            at = slice(k * p.nq // parts, (k + 1) * p.nq // parts)
-            for s in range(at.start, at.stop):
-                held[s] = flat[s * p.ret_pitch : s * p.ret_pitch + p.ret, :].astype(BF)
-            copies.append(pltpu.make_async_copy(held.at[at], out_ref.at[at], sems.at[k]))
-            copies[-1].start()
+        for g in range(p.full):
+            for yl in range(p.nyl):
+                put(g * p.nyl + yl, part(g * p.nyl + yl))
+            copies.append(store(g))
+        for u in range(p.ntail):
+            put(chunks + u, part(chunks + u))
+        copies.append(store(p.full))
         for copy in copies:
             copy.wait()
 
@@ -326,15 +339,11 @@
     def _():
         for r in range(tail + p.ntail * p.c, tail + p.tail):
             flat[pl.ds(r, p.nq, stride=p.ret_pitch), :] = jnp.zeros((p.nq, LANES), F32)
-        for k in range(chunks + p.ntail):
-            put_in_y(k, part(k))
-        store()
+        run(put_in_y)
 
     @pl.when(jnp.logical_not(first))
     def _():
-        for k in range(chunks + p.ntail):
-            put_in_z(k, part(k))
-        store()
+        run(put_in_z)
 
 
 def combine_kernel(p, in_ref, pick_ref, ends_ref, out_ref):
@@ -508,11 +517,12 @@
         out_spaces={0: HBM},
     )
     received = all_to_all(sent, plane_groups)
-    rows_x, partial = call(
+    rows_x, partial, crossing = call(
         bind(project_kernel, p),
         [
             ((p.rows, p.half_d), BF),
             ((p.rows, 6 * LANES), F32),
+            ((p.rows, 6 * LANES), BF),
         ],
         (received, wgu, wd),
         scratch=[
@@ -527,11 +537,11 @@
     back, d_all = call(
         bind(back_kernel, p),
         [((p.nq, p.ret, LANES), BF), ((p.rows, 4 * LANES), BF)],
-        (partial, exchange(partial), wgu),
+        (partial, exchange(crossing), wgu),
         scratch=[
             pltpu.VMEM(((p.nq + 1) * p.ret_pitch, LANES), F32),
             pltpu.VMEM((p.nq, p.ret, LANES), BF),
-            pltpu.SemaphoreType.DMA((4,)),
+            pltpu.SemaphoreType.DMA((p.full + 1,)),
         ],
         out_spaces={0: HBM},
     )

time: 100 us -> 99.5 us (level)
  no operation moved by 1% of the time
where the time goes in v2:
time: 99.5 us; the launch traced here: 98.7 us
  waiting for transfers between devices  41.3 us (42%)
  starting transfers between devices  36.5 us (37%)
  Pallas kernels  12.9 us (13%)
  local copies, waits for them, and re-layouts  6.27 us (6%)
    all_to_all x4, waiting for transfers between devices, all_to_all(): lax.all_to_all(v, AXES, split_axis=0, concat_axis=0, axis_index_groups=gr...  39.7 us
    all_to_all x4, starting transfers between devices, all_to_all(): lax.all_to_all(v, AXES, split_axis=0, concat_axis=0, axis_index_groups=gr...  28.6 us
    pallas_call x9, Pallas kernels, call(): pl.pallas_call(kernel, out_shape=shapes, in_specs=[spaces.get(k, vm) for...  12.9 us
    ppermute x3, starting transfers between devices, exchange(): return lax.ppermute(v, 'core', swap)  7.87 us
    squeeze x2, local copies, waits for them, and re-layouts, program(): wd = lane_tiles(p, jnp.concatenate([mine[2], theirs[2]], axis=-1))  2.45 us
  transfers between devices with their start and end apart: 7, of which 5 were waited for; matrix products, arithmetic and copies ran while one was open for 7% of the time, Pallas kernels for 7%

profile of v2, /device:TPU:64, one launch (start us, length us, event | category | flops | bytes accessed | tf_op | source)
XLA Modules:
  0.0 98.7 jit_solution(14814152143929913870)
XLA Ops:
  0.6 1.7 %shard_map.94 = bf16[8,128,128]{2,1,0:T(8,128)(2,1)} custom-call(bf16[16,448]{1,0:T(8,128)(2,1)} %refs_0_.1, bf16[16,448]{1,0:T(8,128)(2,1)} %refs_1_.1, s32[8,16]{1,0:T(8,128)} %bitcast.46, bf16[8,16]{1,0:T(8,128)(2,1)} %bitcast.47), custom_call_target="tpu_custom_call" | custom-call | bytes 291584 | tf_op jit(solution)/shard_map/pallas_call | solution.py:89
  2.3 0.0 copy-start.3
  2.3 0.0 copy-start.4
  2.3 7.2 %all-to-all-start = ((bf16[8,128,128]{2,1,0:T(8,128)(2,1)}), bf16[8,128,128]{2,1,0:T(8,128)(2,1)S(1)}, u32[]{:S(2)}, u32[]{:S(2)}) async-start(bf16[8,128,128]{2,1,0:T(8,128)(2,1)} %shard_map.94), calls=%async_computation | async-start | bytes 524288 | tf_op jit(solution)/shard_map/all_to_all | solution.py:466
  9.6 1.5 %copy.15 = bf16[1,128,3584]{1,2,0:T(8,128)(2,1)S(1)} copy(bf16[1,128,3584]{2,1,0:T(8,128)(2,1)} %param.13) | data formatting | bytes 1835008 | tf_op jit(solution)/shard_map/optimization_barrier | solution.py:490
  11.1 0.0 copy-done.3
  11.1 0.0 copy-done.4
  11.2 0.3 pad_maximum_fusion
  11.5 0.0 copy-start.2
  11.5 1.5 %dynamic-slice_bitcast_fusion.1 = (bf16[3,4,1,448,128]{4,3,1,2,0:T(8,128)(2,1)S(1)}, bf16[3,4,448,128]{3,2,1,0:T(8,128)(2,1)}) fusion(bf16[3,4,2,448,128]{4,3,2,1,0:T(8,128)(2,1)S(1)} %pad_maximum_fusion, s32[]{:T(128)S(6)} %select_n.7, s32[]{:T(128)S(6)} %select_n.8), kind=kLoop, calls=%fused_computation.4 | loop fusion | bytes 5505032 | tf_op jit(solution)/shard_map/jit(dynamic_index_in_dim)/dynamic_slice | solution.py:495
  13.0 0.4 copy-done.2
  13.4 4.0 %collective-permute-start = (bf16[3,4,448,128]{3,2,1,0:T(8,128)(2,1)}, bf16[3,4,448,128]{3,2,1,0:T(8,128)(2,1)}, u32[]{:S(2)}, u32[]{:S(2)}) collective-permute-start(bf16[3,4,448,128]{3,2,1,0:T(8,128)(2,1)} %get-tuple-element.44), channel_id=1, source_target_pairs={{0,1},{1,0},{2,3},{3,2},{4,5},{5,4},{6,7},{7,6},{8,9},{9,8},{10,11... | collective-permute-start | bytes 4128776 | tf_op jit(solution)/shard_map/ppermute | solution.py:463
  17.4 2.6 %all-to-all-done.in_ref = bf16[8,128,128]{2,1,0:T(8,128)(2,1)S(1)} async-done(((bf16[8,128,128]{2,1,0:T(8,128)(2,1)}), bf16[8,128,128]{2,1,0:T(8,128)(2,1)S(1)}, u32[]{:S(2)}, u32[]{:S(2)}) %all-to-all-start) | async-done | bytes 262176 | tf_op jit(solution)/shard_map/all_to_all | solution.py:466
  20.1 1.7 %shard_map.95 = (bf16[32,168,128]{2,1,0:T(8,128)(2,1)}, f32[32,128]{1,0:T(8,128)S(1)}) custom-call(bf16[8,128,128]{2,1,0:T(8,128)(2,1)S(1)} %all-to-all-done.in_ref), custom_call_target="tpu_custom_call" | custom-call | bytes 1654784 | tf_op jit(solution)/shard_map/pallas_call | solution.py:89
  21.7 12.6 %all-to-all-start.1 = ((bf16[32,168,128]{2,1,0:T(8,128)(2,1)}), bf16[32,168,128]{2,1,0:T(8,128)(2,1)S(1)}, u32[]{:S(2)}, u32[]{:S(2)}) async-start(bf16[32,168,128]{2,1,0:T(8,128)(2,1)} %get-tuple-element.23), calls=%async_computation.1 | async-start | bytes 2752512 | tf_op jit(solution)/shard_map/all_to_all | solution.py:466
  34.3 1.1 %dynamic-slice_bitcast_fusion.2 = bf16[4,448,128]{2,1,0:T(8,128)(2,1)S(1)} fusion(bf16[3,4,2,448,128]{4,3,2,1,0:T(8,128)(2,1)} %copy-done.2, s32[]{:T(128)S(6)} %add.10, s32[]{:T(128)S(6)} %select_n.7), kind=kLoop, calls=%fused_computation.10 | loop fusion | bytes 917512 | tf_op jit(solution)/shard_map/squeeze | solution.py:499
  35.4 0.1 slice_bitcast_fusion.4
  35.5 0.0 collective-permute-done
  35.5 1.4 %slice_bitcast_fusion = (bf16[4,448,128]{2,1,0:T(8,128)(2,1)S(1)}, bf16[4,448,128]{2,1,0:T(8,128)(2,1)S(1)}, bf16[4,448,128]{2,1,0:T(8,128)(2,1)S(1)}) fusion(bf16[3,4,448,128]{3,2,1,0:T(8,128)(2,1)} %collective-permute-done), kind=kLoop, calls=%fused_computation.9 | loop fusion | bytes 2752512 | tf_op jit(solution)/shard_map/squeeze | solution.py:499
  36.9 0.1 fusion
  37.0 0.1 copy.19
  37.0 0.2 pad_maximum_fusion.1
  37.2 0.1 slice.47
  37.4 0.1 copy.18
  37.5 0.1 pad_maximum_fusion.3.in_ref
  37.6 0.9 shard_map.96.wd_hbm
  38.6 0.1 pad_maximum_fusion.2.wgu_ref
  38.7 17.9 %all-to-all-done.1.in_ref = bf16[32,168,128]{2,1,0:T(8,128)(2,1)S(1)} async-done(((bf16[32,168,128]{2,1,0:T(8,128)(2,1)}), bf16[32,168,128]{2,1,0:T(8,128)(2,1)S(1)}, u32[]{:S(2)}, u32[]{:S(2)}) %all-to-all-start.1) | async-done | bytes 1376288 | tf_op jit(solution)/shard_map/all_to_all | solution.py:466
  56.6 1.8 %shard_map.97 = (bf16[192,1792]{1,0:T(8,128)(2,1)S(1)}, f32[192,768]{1,0:T(8,128)S(1)}, bf16[192,768]{1,0:T(8,128)(2,1)S(1)}) custom-call(bf16[32,168,128]{2,1,0:T(8,128)(2,1)S(1)} %all-to-all-done.1.in_ref, bf16[1792,512]{1,0:T(8,128)(2,1)S(1)} %pad_maximum_fusion.2.wgu_ref, bf16[40960,256]{1,0:T(8,128)(2,1)} %shard_map.96.wd_hbm), custom_call_target="tpu_custom_call" | custom-call | bytes 25755648 | tf_op jit(solution)/shard_map/pallas_call | solution.py:89
  58.4 0.0 copy-start
  58.4 1.9 %collective-permute-start.1 = (bf16[192,768]{1,0:T(8,128)(2,1)S(1)}, bf16[192,768]{1,0:T(8,128)(2,1)S(1)}, u32[]{:S(2)}, u32[]{:S(2)}) collective-permute-start(bf16[192,768]{1,0:T(8,128)(2,1)S(1)} %get-tuple-element.28), channel_id=1, source_target_pairs={{0,1},{1,0},{2,3},{3,2},{4,5},{5,4},{6,7},{7,6},{8,9},{9,8},{10,11... | collective-permute-start | bytes 884744 | tf_op jit(solution)/shard_map/ppermute | solution.py:463
  60.3 1.5 %collective-permute-done.1.got_ref = bf16[192,768]{1,0:T(8,128)(2,1)S(1)} collective-permute-done((bf16[192,768]{1,0:T(8,128)(2,1)S(1)}, bf16[192,768]{1,0:T(8,128)(2,1)S(1)}, u32[]{:S(2)}, u32[]{:S(2)}) %collective-permute-start.1) | collective-permute-done | bytes 294944 | tf_op jit(solution)/shard_map/ppermute | solution.py:463
  61.9 1.7 %shard_map.98 = (bf16[32,88,128]{2,1,0:T(8,128)(2,1)}, bf16[192,512]{1,0:T(8,128)(2,1)S(1)}) custom-call(f32[192,768]{1,0:T(8,128)S(1)} %get-tuple-element.27.pre_ref, bf16[192,768]{1,0:T(8,128)(2,1)S(1)} %collective-permute-done.1.got_ref, bf16[1792,512]{1,0:T(8,128)(2,1)S(1)} %pad_maximum_fusion.2.wgu_ref), custom_call_target="tpu_custom_call" | custom-call | bytes 3637248 | tf_op jit(solution)/shard_map/pallas_call | solution.py:89
  63.6 0.0 copy-done
  63.6 0.0 copy-start.1
  63.7 5.4 %all-to-all-start.2 = ((bf16[32,88,128]{2,1,0:T(8,128)(2,1)}), bf16[32,88,128]{2,1,0:T(8,128)(2,1)S(1)}, u32[]{:S(2)}, u32[]{:S(2)}) async-start(bf16[32,88,128]{2,1,0:T(8,128)(2,1)} %get-tuple-element.29), calls=%async_computation.2 | async-start | bytes 1441792 | tf_op jit(solution)/shard_map/all_to_all | solution.py:466
  69.1 0.0 copy-done.1
  69.1 1.9 %shard_map.99 = (bf16[2,4,448,128]{3,2,1,0:T(8,128)(2,1)S(1)}, bf16[4,448,256]{2,1,0:T(8,128)(2,1)}, bf16[128,768]{1,0:T(8,128)(2,1)S(1)}, bf16[128,768]{1,0:T(8,128)(2,1)S(1)}) custom-call(bf16[192,1792]{1,0:T(8,128)(2,1)S(1)} %copy-done.1, bf16[192,512]{1,0:T(8,128)(2,1)S(1)} %get-tuple-element.33.d_ref, f32[32,128]{1,0:T(8,128)S(1)} %get-tuple-element.34.rank_ref), custom_call_target="tpu_custom_call" | custom-call | bytes 3129344 | tf_op jit(solution)/shard_map/pallas_call | solution.py:89
  70.9 1.9 %collective-permute-start.2 = (bf16[4,448,256]{2,1,0:T(8,128)(2,1)}, bf16[4,448,256]{2,1,0:T(8,128)(2,1)S(1)}, u32[]{:S(2)}, u32[]{:S(2)}) collective-permute-start(bf16[4,448,256]{2,1,0:T(8,128)(2,1)} %get-tuple-element.38), channel_id=1, source_target_pairs={{0,1},{1,0},{2,3},{3,2},{4,5},{5,4},{6,7},{7,6},{8,9},{9,8},{10,11... | collective-permute-start | bytes 2752520 | tf_op jit(solution)/shard_map/ppermute | solution.py:463
  72.8 11.7 %all-to-all-done.2.in_ref = bf16[32,88,128]{2,1,0:T(8,128)(2,1)S(1)} async-done(((bf16[32,88,128]{2,1,0:T(8,128)(2,1)}), bf16[32,88,128]{2,1,0:T(8,128)(2,1)S(1)}, u32[]{:S(2)}, u32[]{:S(2)}) %all-to-all-start.2) | async-done | bytes 720928 | tf_op jit(solution)/shard_map/all_to_all | solution.py:466
  84.5 1.1 %shard_map.100 = bf16[8,64,128]{2,1,0:T(8,128)(2,1)} custom-call(bf16[32,88,128]{2,1,0:T(8,128)(2,1)S(1)} %all-to-all-done.2.in_ref, bf16[128,768]{1,0:T(8,128)(2,1)S(1)} %get-tuple-element.35.pick_ref, bf16[128,768]{1,0:T(8,128)(2,1)S(1)} %get-tuple-element.36.ends_ref), custom_call_target="tpu_custom_call" | custom-call | bytes 1245184 | tf_op jit(solution)/shard_map/pallas_call | solution.py:89
  85.7 3.4 %all-to-all-start.3 = ((bf16[8,64,128]{2,1,0:T(8,128)(2,1)}), bf16[8,64,128]{2,1,0:T(8,128)(2,1)S(1)}, u32[]{:S(2)}, u32[]{:S(2)}) async-start(bf16[8,64,128]{2,1,0:T(8,128)(2,1)} %shard_map.100), calls=%async_computation.3 | async-start | bytes 262144 | tf_op jit(solution)/shard_map/all_to_all | solution.py:466
  89.0 0.0 collective-permute-done.2.got_ref
  89.1 1.4 %shard_map.102 = (bf16[4,2,448,128]{3,2,1,0:T(8,128)(2,1)}, bf16[4,2,448,128]{3,2,1,0:T(8,128)(2,1)}) custom-call(bf16[2,4,448,128]{3,2,1,0:T(8,128)(2,1)S(1)} %get-tuple-element.39.mine_ref, bf16[4,448,256]{2,1,0:T(8,128)(2,1)S(1)} %collective-permute-done.2.got_ref), custom_call_target="tpu_custom_call" | custom-call | bytes 3670016 | tf_op jit(solution)/shard_map/pallas_call | solution.py:89
  90.5 7.5 %all-to-all-done.3.in_ref = bf16[8,64,128]{2,1,0:T(8,128)(2,1)S(1)} async-done(((bf16[8,64,128]{2,1,0:T(8,128)(2,1)}), bf16[8,64,128]{2,1,0:T(8,128)(2,1)S(1)}, u32[]{:S(2)}, u32[]{:S(2)}) %all-to-all-start.3) | async-done | bytes 131104 | tf_op jit(solution)/shard_map/all_to_all | solution.py:466
  98.0 0.7 shard_map.101
  (2 shorter events, 0.1 us)
Async XLA Ops:
  2.3 8.8 %copy-start.3 = (bf16[1,3584,128]{2,1,0:T(8,128)(2,1)S(1)}, bf16[1,3584,128]{2,1,0:T(8,128)(2,1)}, u32[]{:S(2)}) copy-start(bf16[1,3584,128]{2,1,0:T(8,128)(2,1)} %param.12) | copy-start | bytes 2752516
  2.3 8.8 %copy-start.4 = (bf16[1,3584,128]{2,1,0:T(8,128)(2,1)S(1)}, bf16[1,3584,128]{2,1,0:T(8,128)(2,1)}, u32[]{:S(2)}) copy-start(bf16[1,3584,128]{2,1,0:T(8,128)(2,1)} %param.11) | copy-start | bytes 2752516
  2.3 17.7 %all-to-all-start = ((bf16[8,128,128]{2,1,0:T(8,128)(2,1)}), bf16[8,128,128]{2,1,0:T(8,128)(2,1)S(1)}, u32[]{:S(2)}, u32[]{:S(2)}) async-start(bf16[8,128,128]{2,1,0:T(8,128)(2,1)} %shard_map.94), calls=%async_computation | async-start | bytes 524288 | tf_op jit(solution)/shard_map/all_to_all | solution.py:466
  11.5 1.9 %copy-start.2 = (bf16[3,4,2,448,128]{4,3,2,1,0:T(8,128)(2,1)}, bf16[3,4,2,448,128]{4,3,2,1,0:T(8,128)(2,1)S(1)}, u32[]{:S(2)}) copy-start(bf16[3,4,2,448,128]{4,3,2,1,0:T(8,128)(2,1)S(1)} %pad_maximum_fusion) | copy-start | bytes 8257540
  13.4 22.1 %collective-permute-start = (bf16[3,4,448,128]{3,2,1,0:T(8,128)(2,1)}, bf16[3,4,448,128]{3,2,1,0:T(8,128)(2,1)}, u32[]{:S(2)}, u32[]{:S(2)}) collective-permute-start(bf16[3,4,448,128]{3,2,1,0:T(8,128)(2,1)} %get-tuple-element.44), channel_id=1, source_target_pairs={{0,1},{1,0},{2,3},{3,2},{4,5},{5,4},{6,7},{7,6},{8,9},{9,8},{10,11... | collective-permute-start | bytes 4128776 | tf_op jit(solution)/shard_map/ppermute | solution.py:463
  21.7 34.9 %all-to-all-start.1 = ((bf16[32,168,128]{2,1,0:T(8,128)(2,1)}), bf16[32,168,128]{2,1,0:T(8,128)(2,1)S(1)}, u32[]{:S(2)}, u32[]{:S(2)}) async-start(bf16[32,168,128]{2,1,0:T(8,128)(2,1)} %get-tuple-element.23), calls=%async_computation.1 | async-start | bytes 2752512 | tf_op jit(solution)/shard_map/all_to_all | solution.py:466
  58.4 5.2 %copy-start = (bf16[192,1792]{1,0:T(8,128)(2,1)}, bf16[192,1792]{1,0:T(8,128)(2,1)S(1)}, u32[]{:S(2)}) copy-start(bf16[192,1792]{1,0:T(8,128)(2,1)S(1)} %get-tuple-element.32.x_ref) | copy-start | bytes 2064388
  58.4 3.5 %collective-permute-start.1 = (bf16[192,768]{1,0:T(8,128)(2,1)S(1)}, bf16[192,768]{1,0:T(8,128)(2,1)S(1)}, u32[]{:S(2)}, u32[]{:S(2)}) collective-permute-start(bf16[192,768]{1,0:T(8,128)(2,1)S(1)} %get-tuple-element.28), channel_id=1, source_target_pairs={{0,1},{1,0},{2,3},{3,2},{4,5},{5,4},{6,7},{7,6},{8,9},{9,8},{10,11... | collective-permute-start | bytes 884744 | tf_op jit(solution)/shard_map/ppermute | solution.py:463
  63.6 5.4 %copy-start.1 = (bf16[192,1792]{1,0:T(8,128)(2,1)S(1)}, bf16[192,1792]{1,0:T(8,128)(2,1)}, u32[]{:S(2)}) copy-start(bf16[192,1792]{1,0:T(8,128)(2,1)} %copy-done) | copy-start | bytes 2064388
  63.7 20.9 %all-to-all-start.2 = ((bf16[32,88,128]{2,1,0:T(8,128)(2,1)}), bf16[32,88,128]{2,1,0:T(8,128)(2,1)S(1)}, u32[]{:S(2)}, u32[]{:S(2)}) async-start(bf16[32,88,128]{2,1,0:T(8,128)(2,1)} %get-tuple-element.29), calls=%async_computation.2 | async-start | bytes 1441792 | tf_op jit(solution)/shard_map/all_to_all | solution.py:466
  70.9 18.1 %collective-permute-start.2 = (bf16[4,448,256]{2,1,0:T(8,128)(2,1)}, bf16[4,448,256]{2,1,0:T(8,128)(2,1)S(1)}, u32[]{:S(2)}, u32[]{:S(2)}) collective-permute-start(bf16[4,448,256]{2,1,0:T(8,128)(2,1)} %get-tuple-element.38), channel_id=1, source_target_pairs={{0,1},{1,0},{2,3},{3,2},{4,5},{5,4},{6,7},{7,6},{8,9},{9,8},{10,11... | collective-permute-start | bytes 2752520 | tf_op jit(solution)/shard_map/ppermute | solution.py:463
  85.7 12.4 %all-to-all-start.3 = ((bf16[8,64,128]{2,1,0:T(8,128)(2,1)}), bf16[8,64,128]{2,1,0:T(8,128)(2,1)S(1)}, u32[]{:S(2)}, u32[]{:S(2)}) async-start(bf16[8,64,128]{2,1,0:T(8,128)(2,1)} %shard_map.100), calls=%async_computation.3 | async-start | bytes 262144 | tf_op jit(solution)/shard_map/all_to_all | solution.py:466

commit v3 on v2

--- a/solution.py
+++ b/solution.py
@@ -12,6 +12,7 @@
 AXES = ("x", "yh", "z", "yl", "core")
 LANES = 128
 HALF = 64
+Y_CORE = 1
 VMEM_LIMIT = 16 * 1024 * 1024
 STASH_ROWS = 40 * 1024
 VMEM_ALL = 67043328
@@ -62,16 +63,16 @@
 
     def column_groups(self):
         xs, yhs, zs, yls = map(range, (self.nx, self.nyh, self.nz, self.nyl))
-        first = [[self.device(x, h, z, l, 0) for h in yhs for l in yls] for x in xs for z in zs]
+        first = [[self.device(x, h, z, l, Y_CORE) for h in yhs for l in yls] for x in xs for z in zs]
         second = [
-            [self.device(x, h, z, l, 1) for z in zs] for x in xs for h in yhs for l in yls
+            [self.device(x, h, z, l, 1 - Y_CORE) for z in zs] for x in xs for h in yhs for l in yls
         ]
         return first + second
 
     def plane_groups(self):
         xs, yhs, zs, yls = map(range, (self.nx, self.nyh, self.nz, self.nyl))
-        first = [[self.device(x, h, z, l, 0) for x in xs for z in zs] for h in yhs for l in yls]
-        second = [[self.device(x, h, z, l, 1) for x in xs for h in yhs for l in yls] for z in zs]
+        first = [[self.device(x, h, z, l, Y_CORE) for x in xs for z in zs] for h in yhs for l in yls]
+        second = [[self.device(x, h, z, l, 1 - Y_CORE) for x in xs for h in yhs for l in yls] for z in zs]
         return first + second
 
 
@@ -108,7 +109,7 @@
     for fetch in fetches:
         fetch.wait()
     in_y = lax.axis_index("yh") * p.nyl + lax.axis_index("yl")
-    block = jnp.where(lax.axis_index("core") == 0, in_y, lax.axis_index("z"))
+    block = jnp.where(lax.axis_index("core") == Y_CORE, in_y, lax.axis_index("z"))
     top = p.full * LANES
     low = (iota((HALF, LANES), 1) == iota((HALF, LANES), 0)).astype(BF)
     high = (iota((HALF, LANES), 1) == iota((HALF, LANES), 0) + HALF).astype(BF)
@@ -151,7 +152,7 @@
 
 
 def dispatch_kernel(p, in_ref, out_ref, rank_ref, held, sems):
-    first = lax.axis_index("core") == 0
+    first = lax.axis_index("core") == Y_CORE
     yh, z = lax.axis_index("yh"), lax.axis_index("z")
     t = p.tok
     meta = in_ref[0, p.groups * t :, :].astype(F32)
@@ -196,7 +197,7 @@
 def project_kernel(p, in_ref, wgu_ref, wd_hbm, x_ref, pre_ref, send_ref, flat, dy, wd, sem):
     fetch = pltpu.make_async_copy(wd_hbm.at[: p.half_d], wd, sem)
     fetch.start()
-    first = lax.axis_index("core") == 0
+    first = lax.axis_index("core") == Y_CORE
 
     def piece_in_y(group, yl):
         row = group * p.grp + yl * p.c
@@ -333,7 +334,7 @@
         for copy in copies:
             copy.wait()
 
-    first = lax.axis_index("core") == 0
+    first = lax.axis_index("core") == Y_CORE
 
     @pl.when(first)
     def _():
@@ -348,7 +349,7 @@
 
 def combine_kernel(p, in_ref, pick_ref, ends_ref, out_ref):
     t = p.tok
-    first = lax.axis_index("core") == 0
+    first = lax.axis_index("core") == Y_CORE
     for g in range(p.full):
         rows = in_ref[:, g * p.grp : (g + 1) * p.grp, :].reshape(p.nq * p.grp, LANES)
         total = jnp.dot(pick_ref[...], rows, preferred_element_type=F32)
@@ -378,7 +379,7 @@
 
 
 def finish_kernel(p, in_ref, out_ref):
-    odd = jnp.where(lax.axis_index("core") == 0, lax.axis_index("yl") % 2, 0)
+    odd = jnp.where(lax.axis_index("core") == Y_CORE, lax.axis_index("yl") % 2, 0)
     total = in_ref[0].astype(F32)
     for b in range(1, p.nb):
         total = total + in_ref[b].astype(F32)
@@ -391,7 +392,7 @@
 
 
 def grads_kernel(p, x_ref, d_ref, rank_ref, mine_ref, other_ref, pick_ref, ends_ref):
-    first = lax.axis_index("core") == 0
+    first = lax.axis_index("core") == Y_CORE
     eq = rank_ref[...][:, None, :] == slot_target(p, first)[None, :, :]
     pick = jnp.where(eq, 1.0, 0.0).astype(F32)
 

time: 99.5 us -> 100 us (level)
  the two profiles are of different devices: /device:TPU:64 before, /device:TPU:8 now
where the time goes in v3:
time: 100 us; the launch traced here: 99.4 us
  waiting for transfers between devices  43.3 us (43%)
  starting transfers between devices  35.1 us (35%)
  Pallas kernels  13 us (13%)
  local copies, waits for them, and re-layouts  6.27 us (6%)
    all_to_all x4, waiting for transfers between devices, all_to_all(): lax.all_to_all(v, AXES, split_axis=0, concat_axis=0, axis_index_groups=gr...  41.8 us
    all_to_all x4, starting transfers between devices, all_to_all(): lax.all_to_all(v, AXES, split_axis=0, concat_axis=0, axis_index_groups=gr...  29.4 us
    pallas_call x9, Pallas kernels, call(): pl.pallas_call(kernel, out_shape=shapes, in_specs=[spaces.get(k, vm) for...  13 us
    ppermute x3, starting transfers between devices, exchange(): return lax.ppermute(v, 'core', swap)  5.74 us
    squeeze x2, local copies, waits for them, and re-layouts, program(): wd = lane_tiles(p, jnp.concatenate([mine[2], theirs[2]], axis=-1))  2.45 us
  transfers between devices with their start and end apart: 7, of which 5 were waited for; matrix products, arithmetic and copies ran while one was open for 7% of the time, Pallas kernels for 7%

profile of v3, /device:TPU:8, one launch (start us, length us, event | category | flops | bytes accessed | tf_op | source)
XLA Modules:
  0.0 99.4 jit_solution(13524232053376671235)
XLA Ops:
  0.6 1.7 %shard_map.94 = bf16[8,128,128]{2,1,0:T(8,128)(2,1)} custom-call(bf16[16,448]{1,0:T(8,128)(2,1)} %refs_0_.1, bf16[16,448]{1,0:T(8,128)(2,1)} %refs_1_.1, s32[8,16]{1,0:T(8,128)} %bitcast.46, bf16[8,16]{1,0:T(8,128)(2,1)} %bitcast.47), custom_call_target="tpu_custom_call" | custom-call | bytes 291584 | tf_op jit(solution)/shard_map/pallas_call | solution.py:90
  2.3 0.0 copy-start.3
  2.3 0.0 copy-start.4
  2.3 10.5 %all-to-all-start = ((bf16[8,128,128]{2,1,0:T(8,128)(2,1)}), bf16[8,128,128]{2,1,0:T(8,128)(2,1)S(1)}, u32[]{:S(2)}, u32[]{:S(2)}) async-start(bf16[8,128,128]{2,1,0:T(8,128)(2,1)} %shard_map.94), calls=%async_computation | async-start | bytes 524288 | tf_op jit(solution)/shard_map/all_to_all | solution.py:467
  12.8 1.5 %copy.15 = bf16[1,128,3584]{1,2,0:T(8,128)(2,1)S(1)} copy(bf16[1,128,3584]{2,1,0:T(8,128)(2,1)} %param.13) | data formatting | bytes 1835008 | tf_op jit(solution)/shard_map/optimization_barrier | solution.py:491
  14.3 0.0 copy-done.3
  14.4 0.0 copy-done.4
  14.4 0.3 pad_maximum_fusion
  14.7 0.0 copy-start.2
  14.7 1.5 %dynamic-slice_bitcast_fusion.1 = (bf16[3,4,1,448,128]{4,3,1,2,0:T(8,128)(2,1)S(1)}, bf16[3,4,448,128]{3,2,1,0:T(8,128)(2,1)}) fusion(bf16[3,4,2,448,128]{4,3,2,1,0:T(8,128)(2,1)S(1)} %pad_maximum_fusion, s32[]{:T(128)S(6)} %select_n.7, s32[]{:T(128)S(6)} %select_n.8), kind=kLoop, calls=%fused_computation.4 | loop fusion | bytes 5505032 | tf_op jit(solution)/shard_map/jit(dynamic_index_in_dim)/dynamic_slice | solution.py:496
  16.2 0.4 copy-done.2
  16.6 1.9 %collective-permute-start = (bf16[3,4,448,128]{3,2,1,0:T(8,128)(2,1)}, bf16[3,4,448,128]{3,2,1,0:T(8,128)(2,1)}, u32[]{:S(2)}, u32[]{:S(2)}) collective-permute-start(bf16[3,4,448,128]{3,2,1,0:T(8,128)(2,1)} %get-tuple-element.44), channel_id=1, source_target_pairs={{0,1},{1,0},{2,3},{3,2},{4,5},{5,4},{6,7},{7,6},{8,9},{9,8},{10,11... | collective-permute-start | bytes 4128776 | tf_op jit(solution)/shard_map/ppermute | solution.py:464
  18.5 4.7 %all-to-all-done.in_ref = bf16[8,128,128]{2,1,0:T(8,128)(2,1)S(1)} async-done(((bf16[8,128,128]{2,1,0:T(8,128)(2,1)}), bf16[8,128,128]{2,1,0:T(8,128)(2,1)S(1)}, u32[]{:S(2)}, u32[]{:S(2)}) %all-to-all-start) | async-done | bytes 262176 | tf_op jit(solution)/shard_map/all_to_all | solution.py:467
  23.3 1.7 %shard_map.95 = (bf16[32,168,128]{2,1,0:T(8,128)(2,1)}, f32[32,128]{1,0:T(8,128)S(1)}) custom-call(bf16[8,128,128]{2,1,0:T(8,128)(2,1)S(1)} %all-to-all-done.in_ref), custom_call_target="tpu_custom_call" | custom-call | bytes 1654784 | tf_op jit(solution)/shard_map/pallas_call | solution.py:90
  24.9 10.2 %all-to-all-start.1 = ((bf16[32,168,128]{2,1,0:T(8,128)(2,1)}), bf16[32,168,128]{2,1,0:T(8,128)(2,1)S(1)}, u32[]{:S(2)}, u32[]{:S(2)}) async-start(bf16[32,168,128]{2,1,0:T(8,128)(2,1)} %get-tuple-element.23), calls=%async_computation.1 | async-start | bytes 2752512 | tf_op jit(solution)/shard_map/all_to_all | solution.py:467
  35.1 1.1 %dynamic-slice_bitcast_fusion.2 = bf16[4,448,128]{2,1,0:T(8,128)(2,1)S(1)} fusion(bf16[3,4,2,448,128]{4,3,2,1,0:T(8,128)(2,1)} %copy-done.2, s32[]{:T(128)S(6)} %add.10, s32[]{:T(128)S(6)} %select_n.7), kind=kLoop, calls=%fused_computation.10 | loop fusion | bytes 917512 | tf_op jit(solution)/shard_map/squeeze | solution.py:500
  36.2 0.1 slice_bitcast_fusion.4
  36.3 0.0 collective-permute-done
  36.3 1.4 %slice_bitcast_fusion = (bf16[4,448,128]{2,1,0:T(8,128)(2,1)S(1)}, bf16[4,448,128]{2,1,0:T(8,128)(2,1)S(1)}, bf16[4,448,128]{2,1,0:T(8,128)(2,1)S(1)}) fusion(bf16[3,4,448,128]{3,2,1,0:T(8,128)(2,1)} %collective-permute-done), kind=kLoop, calls=%fused_computation.9 | loop fusion | bytes 2752512 | tf_op jit(solution)/shard_map/squeeze | solution.py:500
  37.7 0.1 fusion
  37.8 0.1 copy.19
  37.8 0.2 pad_maximum_fusion.1
  38.0 0.1 slice.47
  38.2 0.1 copy.18
  38.3 0.1 pad_maximum_fusion.3.in_ref
  38.4 0.9 shard_map.96.wd_hbm
  39.4 0.1 pad_maximum_fusion.2.wgu_ref
  39.5 17.8 %all-to-all-done.1.in_ref = bf16[32,168,128]{2,1,0:T(8,128)(2,1)S(1)} async-done(((bf16[32,168,128]{2,1,0:T(8,128)(2,1)}), bf16[32,168,128]{2,1,0:T(8,128)(2,1)S(1)}, u32[]{:S(2)}, u32[]{:S(2)}) %all-to-all-start.1) | async-done | bytes 1376288 | tf_op jit(solution)/shard_map/all_to_all | solution.py:467
  57.3 1.7 %shard_map.97 = (bf16[192,1792]{1,0:T(8,128)(2,1)S(1)}, f32[192,768]{1,0:T(8,128)S(1)}, bf16[192,768]{1,0:T(8,128)(2,1)S(1)}) custom-call(bf16[32,168,128]{2,1,0:T(8,128)(2,1)S(1)} %all-to-all-done.1.in_ref, bf16[1792,512]{1,0:T(8,128)(2,1)S(1)} %pad_maximum_fusion.2.wgu_ref, bf16[40960,256]{1,0:T(8,128)(2,1)} %shard_map.96.wd_hbm), custom_call_target="tpu_custom_call" | custom-call | bytes 25755648 | tf_op jit(solution)/shard_map/pallas_call | solution.py:90
  59.0 0.0 copy-start
  59.0 1.9 %collective-permute-start.1 = (bf16[192,768]{1,0:T(8,128)(2,1)S(1)}, bf16[192,768]{1,0:T(8,128)(2,1)S(1)}, u32[]{:S(2)}, u32[]{:S(2)}) collective-permute-start(bf16[192,768]{1,0:T(8,128)(2,1)S(1)} %get-tuple-element.28), channel_id=1, source_target_pairs={{0,1},{1,0},{2,3},{3,2},{4,5},{5,4},{6,7},{7,6},{8,9},{9,8},{10,11... | collective-permute-start | bytes 884744 | tf_op jit(solution)/shard_map/ppermute | solution.py:464
  61.0 1.5 %collective-permute-done.1.got_ref = bf16[192,768]{1,0:T(8,128)(2,1)S(1)} collective-permute-done((bf16[192,768]{1,0:T(8,128)(2,1)S(1)}, bf16[192,768]{1,0:T(8,128)(2,1)S(1)}, u32[]{:S(2)}, u32[]{:S(2)}) %collective-permute-start.1) | collective-permute-done | bytes 294944 | tf_op jit(solution)/shard_map/ppermute | solution.py:464
  62.5 1.8 %shard_map.98 = (bf16[32,88,128]{2,1,0:T(8,128)(2,1)}, bf16[192,512]{1,0:T(8,128)(2,1)S(1)}) custom-call(f32[192,768]{1,0:T(8,128)S(1)} %get-tuple-element.27.pre_ref, bf16[192,768]{1,0:T(8,128)(2,1)S(1)} %collective-permute-done.1.got_ref, bf16[1792,512]{1,0:T(8,128)(2,1)S(1)} %pad_maximum_fusion.2.wgu_ref), custom_call_target="tpu_custom_call" | custom-call | bytes 3637248 | tf_op jit(solution)/shard_map/pallas_call | solution.py:90
  64.3 0.0 copy-done
  64.3 0.0 copy-start.1
  64.3 5.3 %all-to-all-start.2 = ((bf16[32,88,128]{2,1,0:T(8,128)(2,1)}), bf16[32,88,128]{2,1,0:T(8,128)(2,1)S(1)}, u32[]{:S(2)}, u32[]{:S(2)}) async-start(bf16[32,88,128]{2,1,0:T(8,128)(2,1)} %get-tuple-element.29), calls=%async_computation.2 | async-start | bytes 1441792 | tf_op jit(solution)/shard_map/all_to_all | solution.py:467
  69.7 0.0 copy-done.1
  69.7 1.9 %shard_map.99 = (bf16[2,4,448,128]{3,2,1,0:T(8,128)(2,1)S(1)}, bf16[4,448,256]{2,1,0:T(8,128)(2,1)}, bf16[128,768]{1,0:T(8,128)(2,1)S(1)}, bf16[128,768]{1,0:T(8,128)(2,1)S(1)}) custom-call(bf16[192,1792]{1,0:T(8,128)(2,1)S(1)} %copy-done.1, bf16[192,512]{1,0:T(8,128)(2,1)S(1)} %get-tuple-element.33.d_ref, f32[32,128]{1,0:T(8,128)S(1)} %get-tuple-element.34.rank_ref), custom_call_target="tpu_custom_call" | custom-call | bytes 3129344 | tf_op jit(solution)/shard_map/pallas_call | solution.py:90
  71.6 1.9 %collective-permute-start.2 = (bf16[4,448,256]{2,1,0:T(8,128)(2,1)}, bf16[4,448,256]{2,1,0:T(8,128)(2,1)S(1)}, u32[]{:S(2)}, u32[]{:S(2)}) collective-permute-start(bf16[4,448,256]{2,1,0:T(8,128)(2,1)} %get-tuple-element.38), channel_id=1, source_target_pairs={{0,1},{1,0},{2,3},{3,2},{4,5},{5,4},{6,7},{7,6},{8,9},{9,8},{10,11... | collective-permute-start | bytes 2752520 | tf_op jit(solution)/shard_map/ppermute | solution.py:464
  73.5 11.6 %all-to-all-done.2.in_ref = bf16[32,88,128]{2,1,0:T(8,128)(2,1)S(1)} async-done(((bf16[32,88,128]{2,1,0:T(8,128)(2,1)}), bf16[32,88,128]{2,1,0:T(8,128)(2,1)S(1)}, u32[]{:S(2)}, u32[]{:S(2)}) %all-to-all-start.2) | async-done | bytes 720928 | tf_op jit(solution)/shard_map/all_to_all | solution.py:467
  85.1 1.2 %shard_map.100 = bf16[8,64,128]{2,1,0:T(8,128)(2,1)} custom-call(bf16[32,88,128]{2,1,0:T(8,128)(2,1)S(1)} %all-to-all-done.2.in_ref, bf16[128,768]{1,0:T(8,128)(2,1)S(1)} %get-tuple-element.35.pick_ref, bf16[128,768]{1,0:T(8,128)(2,1)S(1)} %get-tuple-element.36.ends_ref), custom_call_target="tpu_custom_call" | custom-call | bytes 1245184 | tf_op jit(solution)/shard_map/pallas_call | solution.py:90
  86.3 3.4 %all-to-all-start.3 = ((bf16[8,64,128]{2,1,0:T(8,128)(2,1)}), bf16[8,64,128]{2,1,0:T(8,128)(2,1)S(1)}, u32[]{:S(2)}, u32[]{:S(2)}) async-start(bf16[8,64,128]{2,1,0:T(8,128)(2,1)} %shard_map.100), calls=%async_computation.3 | async-start | bytes 262144 | tf_op jit(solution)/shard_map/all_to_all | solution.py:467
  89.7 0.0 collective-permute-done.2.got_ref
  89.7 1.4 %shard_map.102 = (bf16[4,2,448,128]{3,2,1,0:T(8,128)(2,1)}, bf16[4,2,448,128]{3,2,1,0:T(8,128)(2,1)}) custom-call(bf16[2,4,448,128]{3,2,1,0:T(8,128)(2,1)S(1)} %get-tuple-element.39.mine_ref, bf16[4,448,256]{2,1,0:T(8,128)(2,1)S(1)} %collective-permute-done.2.got_ref), custom_call_target="tpu_custom_call" | custom-call | bytes 3670016 | tf_op jit(solution)/shard_map/pallas_call | solution.py:90
  91.2 7.5 %all-to-all-done.3.in_ref = bf16[8,64,128]{2,1,0:T(8,128)(2,1)S(1)} async-done(((bf16[8,64,128]{2,1,0:T(8,128)(2,1)}), bf16[8,64,128]{2,1,0:T(8,128)(2,1)S(1)}, u32[]{:S(2)}, u32[]{:S(2)}) %all-to-all-start.3) | async-done | bytes 131104 | tf_op jit(solution)/shard_map/all_to_all | solution.py:467
  98.7 0.7 shard_map.101
  (2 shorter events, 0.1 us)
Async XLA Ops:
  2.3 12.0 %copy-start.3 = (bf16[1,3584,128]{2,1,0:T(8,128)(2,1)S(1)}, bf16[1,3584,128]{2,1,0:T(8,128)(2,1)}, u32[]{:S(2)}) copy-start(bf16[1,3584,128]{2,1,0:T(8,128)(2,1)} %param.12) | copy-start | bytes 2752516
  2.3 12.0 %copy-start.4 = (bf16[1,3584,128]{2,1,0:T(8,128)(2,1)S(1)}, bf16[1,3584,128]{2,1,0:T(8,128)(2,1)}, u32[]{:S(2)}) copy-start(bf16[1,3584,128]{2,1,0:T(8,128)(2,1)} %param.11) | copy-start | bytes 2752516
  2.3 20.9 %all-to-all-start = ((bf16[8,128,128]{2,1,0:T(8,128)(2,1)}), bf16[8,128,128]{2,1,0:T(8,128)(2,1)S(1)}, u32[]{:S(2)}, u32[]{:S(2)}) async-start(bf16[8,128,128]{2,1,0:T(8,128)(2,1)} %shard_map.94), calls=%async_computation | async-start | bytes 524288 | tf_op jit(solution)/shard_map/all_to_all | solution.py:467
  14.7 1.9 %copy-start.2 = (bf16[3,4,2,448,128]{4,3,2,1,0:T(8,128)(2,1)}, bf16[3,4,2,448,128]{4,3,2,1,0:T(8,128)(2,1)S(1)}, u32[]{:S(2)}) copy-start(bf16[3,4,2,448,128]{4,3,2,1,0:T(8,128)(2,1)S(1)} %pad_maximum_fusion) | copy-start | bytes 8257540
  16.6 19.7 %collective-permute-start = (bf16[3,4,448,128]{3,2,1,0:T(8,128)(2,1)}, bf16[3,4,448,128]{3,2,1,0:T(8,128)(2,1)}, u32[]{:S(2)}, u32[]{:S(2)}) collective-permute-start(bf16[3,4,448,128]{3,2,1,0:T(8,128)(2,1)} %get-tuple-element.44), channel_id=1, source_target_pairs={{0,1},{1,0},{2,3},{3,2},{4,5},{5,4},{6,7},{7,6},{8,9},{9,8},{10,11... | collective-permute-start | bytes 4128776 | tf_op jit(solution)/shard_map/ppermute | solution.py:464
  24.9 32.4 %all-to-all-start.1 = ((bf16[32,168,128]{2,1,0:T(8,128)(2,1)}), bf16[32,168,128]{2,1,0:T(8,128)(2,1)S(1)}, u32[]{:S(2)}, u32[]{:S(2)}) async-start(bf16[32,168,128]{2,1,0:T(8,128)(2,1)} %get-tuple-element.23), calls=%async_computation.1 | async-start | bytes 2752512 | tf_op jit(solution)/shard_map/all_to_all | solution.py:467
  59.0 5.3 %copy-start = (bf16[192,1792]{1,0:T(8,128)(2,1)}, bf16[192,1792]{1,0:T(8,128)(2,1)S(1)}, u32[]{:S(2)}) copy-start(bf16[192,1792]{1,0:T(8,128)(2,1)S(1)} %get-tuple-element.32.x_ref) | copy-start | bytes 2064388
  59.0 3.5 %collective-permute-start.1 = (bf16[192,768]{1,0:T(8,128)(2,1)S(1)}, bf16[192,768]{1,0:T(8,128)(2,1)S(1)}, u32[]{:S(2)}, u32[]{:S(2)}) collective-permute-start(bf16[192,768]{1,0:T(8,128)(2,1)S(1)} %get-tuple-element.28), channel_id=1, source_target_pairs={{0,1},{1,0},{2,3},{3,2},{4,5},{5,4},{6,7},{7,6},{8,9},{9,8},{10,11... | collective-permute-start | bytes 884744 | tf_op jit(solution)/shard_map/ppermute | solution.py:464
  64.3 5.4 %copy-start.1 = (bf16[192,1792]{1,0:T(8,128)(2,1)S(1)}, bf16[192,1792]{1,0:T(8,128)(2,1)}, u32[]{:S(2)}) copy-start(bf16[192,1792]{1,0:T(8,128)(2,1)} %copy-done) | copy-start | bytes 2064388
  64.3 20.8 %all-to-all-start.2 = ((bf16[32,88,128]{2,1,0:T(8,128)(2,1)}), bf16[32,88,128]{2,1,0:T(8,128)(2,1)S(1)}, u32[]{:S(2)}, u32[]{:S(2)}) async-start(bf16[32,88,128]{2,1,0:T(8,128)(2,1)} %get-tuple-element.29), calls=%async_computation.2 | async-start | bytes 1441792 | tf_op jit(solution)/shard_map/all_to_all | solution.py:467
  71.6 18.1 %collective-permute-start.2 = (bf16[4,448,256]{2,1,0:T(8,128)(2,1)}, bf16[4,448,256]{2,1,0:T(8,128)(2,1)S(1)}, u32[]{:S(2)}, u32[]{:S(2)}) collective-permute-start(bf16[4,448,256]{2,1,0:T(8,128)(2,1)} %get-tuple-element.38), channel_id=1, source_target_pairs={{0,1},{1,0},{2,3},{3,2},{4,5},{5,4},{6,7},{7,6},{8,9},{9,8},{10,11... | collective-permute-start | bytes 2752520 | tf_op jit(solution)/shard_map/ppermute | solution.py:464
  86.3 12.4 %all-to-all-start.3 = ((bf16[8,64,128]{2,1,0:T(8,128)(2,1)}), bf16[8,64,128]{2,1,0:T(8,128)(2,1)S(1)}, u32[]{:S(2)}, u32[]{:S(2)}) async-start(bf16[8,64,128]{2,1,0:T(8,128)(2,1)} %shard_map.100), calls=%async_computation.3 | async-start | bytes 262144 | tf_op jit(solution)/shard_map/all_to_all | solution.py:467
